TPU v7x, 32 devices: a whole 2x2x4 slice. The times are simulated.
32 devices in a mesh: ctx: 16 (over z, x, core), fsdp: 2 (over y).
Axes of the slice: x: 2, y: 2, z: 4, core: 2. Of those that a mesh axis runs over, the one named last changes fastest.
Arguments:
- tokens: bfloat16 [2, 4096, 768], P('fsdp', 'ctx'), may hold values from -6 to 6
- timestep: int32 [2, 16], P('fsdp', 'ctx'), may hold values from 0 to 1023
- time_table: float32 [1024, 768], replicated, may hold values from -2 to 2
- w_qkv: bfloat16 [768, 2304], P('fsdp'), may hold values from -0.21875 to 0.21875
- w_out: bfloat16 [768, 768], P('fsdp'), may hold values from -2.5 to 2.5
- w_up: bfloat16 [768, 3072], P('fsdp'), may hold values from -0.21875 to 0.21875
- w_down: bfloat16 [3072, 768], P('fsdp'), may hold values from -0.3125 to 0.3125
- w_ada: bfloat16 [768, 3072], P('fsdp'), may hold values from -0.21875 to 0.21875
- cotangent: bfloat16 [2, 4096, 768], P('fsdp', 'ctx'), may hold values from -6 to 6
Outputs:
- output: float32 [2, 4096, 768], P('fsdp', 'ctx')
- input_grad: float32 [2, 4096, 768], P('fsdp', 'ctx')
- grad_qkv: float32 [768, 2304], P('fsdp')
- grad_out: float32 [768, 768], P('fsdp')
- grad_up: float32 [768, 3072], P('fsdp')
- grad_down: float32 [3072, 768], P('fsdp')
- grad_ada: float32 [768, 3072], P('fsdp')
All inputs are finite; a program needn't handle non-finite values.
Results may differ from a plain program's by a relative error of at most 0.04.
Values may be sent and summed in bfloat16 or wider, within the bound.
A program may use at most 512 MiB of HBM per device.

v0:
```python
import math

import jax
import jax.numpy as jnp
from jax import lax
from jax.sharding import PartitionSpec as P

HD = 64
BLOCK = 256


norm_eps = 1e-06
masked_score = -1e30
rope_base = 10000.0


def layer_norm(values):
    center = values - jnp.mean(values, axis=-1, keepdims=True)
    inverse = lax.rsqrt(jnp.mean(center * center, axis=-1, keepdims=True) + norm_eps)
    return (center * inverse, inverse)


def norm_back(grad_norm, normed, inverse):
    mean_grad = jnp.mean(grad_norm, axis=-1, keepdims=True)
    mean_cross = jnp.mean(grad_norm * normed, axis=-1, keepdims=True)
    return inverse * (grad_norm - mean_grad - normed * mean_cross)


def rope_tables(positions, head_size):
    half_size = head_size // 2
    frequency = jnp.exp(
        jnp.arange(half_size, dtype=jnp.float32) * (-2.0 * math.log(rope_base) / head_size)
    )
    angles = positions.astype(jnp.float32)[:, None] * frequency[None, :]
    cosine_table = jnp.concatenate([jnp.cos(angles), jnp.cos(angles)], axis=-1)[:, None, :]
    sine_table = jnp.concatenate([jnp.sin(angles), jnp.sin(angles)], axis=-1)[:, None, :]
    return (cosine_table, sine_table)


def rotate_half(values):
    middle = values.shape[-1] // 2
    return jnp.concatenate([-values[..., middle:], values[..., :middle]], axis=-1)


def rotate(values, cosine_table, sine_table):
    return values * cosine_table + rotate_half(values) * sine_table


def rotate_back(gradient, cosine_table, sine_table):
    return gradient * cosine_table - rotate_half(gradient * sine_table)


def gelu_tanh(values):
    return jax.nn.gelu(values, approximate=True)


def split_rows(array, sub_rows):
    return array.reshape((array.shape[0] // sub_rows, sub_rows) + array.shape[1:])


def part_starts(total_rows, sub_rows):
    return sub_rows * jnp.arange(total_rows // sub_rows, dtype=jnp.int32)


def keep_same(partial_value):
    return partial_value


def attend_forward(partial_value, pieces, queries, query_block, score_scale):
    key_rows, value_rows = pieces
    sub_rows = queries.shape[0]

    def attend_visit(running, scan_item):
        key_part, value_part, part_start = scan_item

        def attend_update(running):
            running_max, running_sum, running_out = running
            key_block = (part_start + jnp.arange(sub_rows, dtype=jnp.int32)) // BLOCK
            allowed = (key_block[None, :] <= query_block[:, None])[None]
            scores = (
                jnp.einsum("qhd,khd->hqk", queries, key_part, preferred_element_type=jnp.float32)
                * score_scale
            )
            scores = jnp.where(allowed, scores, masked_score)
            new_max = jnp.maximum(running_max, jnp.max(scores, axis=-1))
            weights = jnp.where(allowed, jnp.exp(scores - new_max[..., None]), 0.0)
            decay = jnp.exp(running_max - new_max)
            running_sum = running_sum * decay + jnp.sum(weights, axis=-1)
            running_out = running_out * decay[..., None] + jnp.einsum(
                "hqk,khd->hqd",
                weights.astype(jnp.bfloat16),
                value_part,
                preferred_element_type=jnp.float32,
            )
            return (new_max, running_sum, running_out)

        return (
            lax.cond(part_start // BLOCK <= query_block[-1], attend_update, keep_same, running),
            None,
        )

    partial_value, unused = lax.scan(
        attend_visit,
        partial_value,
        (
            split_rows(key_rows, sub_rows),
            split_rows(value_rows, sub_rows),
            part_starts(key_rows.shape[0], sub_rows),
        ),
    )
    return partial_value


def on_device(tokens, timestep, time_table, w_qkv, w_out, w_up, w_down, w_ada, cotangent):
    tok_rows = tokens.shape[1]
    model_width = tokens.shape[2]
    heads = model_width // HD
    score_scale = 1.0 / math.sqrt(HD)
    highest_precision = lax.Precision.HIGHEST
    full_weights = (
        lax.all_gather(w_qkv, "fsdp", axis=0, tiled=True),
        lax.all_gather(w_out, "fsdp", axis=0, tiled=True),
        lax.all_gather(w_up, "fsdp", axis=0, tiled=True),
        lax.all_gather(w_down, "fsdp", axis=0, tiled=True),
        lax.all_gather(w_ada, "fsdp", axis=0, tiled=True),
    )
    qkv_full, out_full, up_full, down_full, ada_full = full_weights
    steps_onehot = (
        timestep[0][:, None] == jnp.arange(time_table.shape[0], dtype=jnp.int32)[None, :]
    ).astype(jnp.float32)
    embedded = jnp.dot(steps_onehot, time_table, precision=highest_precision).astype(jnp.bfloat16)
    modulation = jnp.dot(embedded, ada_full, preferred_element_type=jnp.float32)
    per_token = jnp.repeat(modulation, BLOCK, axis=0)
    scale_attn, gate_attn, scale_mlp, gate_mlp = jnp.split(per_token, 4, axis=1)
    inputs = tokens[0].astype(jnp.float32)
    normed_one, inverse_one = layer_norm(inputs)
    residual_first = (normed_one * (1.0 + scale_attn)).astype(jnp.bfloat16)
    projected_output = jnp.dot(
        residual_first, qkv_full, preferred_element_type=jnp.float32
    ).reshape(tok_rows, 3, heads, HD)
    positions = lax.axis_index("ctx") * tok_rows + jnp.arange(tok_rows, dtype=jnp.int32)
    cosine_table, sine_table = rope_tables(positions, HD)
    queries = rotate(projected_output[:, 0], cosine_table, sine_table).astype(jnp.bfloat16)
    key_own = rotate(projected_output[:, 1], cosine_table, sine_table).astype(jnp.bfloat16)
    value_own = projected_output[:, 2].astype(jnp.bfloat16)
    query_block = positions // BLOCK
    start_state = (
        jnp.full((heads, tok_rows), masked_score, jnp.float32),
        jnp.zeros((heads, tok_rows), jnp.float32),
        jnp.zeros((heads, tok_rows, HD), jnp.float32),
    )
    running_max, running_sum, running_out = attend_forward(
        start_state,
        (
            lax.all_gather(key_own, "ctx", axis=0, tiled=True),
            lax.all_gather(value_own, "ctx", axis=0, tiled=True),
        ),
        queries,
        query_block,
        score_scale,
    )
    attn_rows = jnp.transpose(running_out / running_sum[..., None], (1, 0, 2))
    query_lse = running_max + jnp.log(running_sum)
    attn_low = attn_rows.reshape(tok_rows, model_width).astype(jnp.bfloat16)
    attention_projected = jnp.dot(attn_low, out_full, preferred_element_type=jnp.float32)
    middle = inputs + gate_attn * attention_projected
    normed_two, inverse_two = layer_norm(middle)
    residual_second = (normed_two * (1.0 + scale_mlp)).astype(jnp.bfloat16)
    before_activation = jnp.dot(residual_second, up_full, preferred_element_type=jnp.float32)
    gelu_activated, gelu_back = jax.vjp(gelu_tanh, before_activation)
    act_low = gelu_activated.astype(jnp.bfloat16)
    feedforward_output = jnp.dot(act_low, down_full, preferred_element_type=jnp.float32)
    result = middle + gate_mlp * feedforward_output
    qkv_back, out_back, up_back, down_back = (
        lax.all_gather(w_qkv, "fsdp", axis=0, tiled=True),
        lax.all_gather(w_out, "fsdp", axis=0, tiled=True),
        lax.all_gather(w_up, "fsdp", axis=0, tiled=True),
        lax.all_gather(w_down, "fsdp", axis=0, tiled=True),
    )
    upstream = cotangent[0].astype(jnp.float32)
    grad_gate_mlp = upstream * feedforward_output
    grad_mlp = (upstream * gate_mlp).astype(jnp.bfloat16)
    grad_down = jnp.einsum("tf,td->fd", act_low, grad_mlp, preferred_element_type=jnp.float32)
    grad_act = jnp.einsum("td,fd->tf", grad_mlp, down_back, preferred_element_type=jnp.float32)
    grad_pre = gelu_back(grad_act)[0].astype(jnp.bfloat16)
    grad_up = jnp.einsum("td,tf->df", residual_second, grad_pre, preferred_element_type=jnp.float32)
    grad_hidden_two = jnp.einsum("tf,df->td", grad_pre, up_back, preferred_element_type=jnp.float32)
    grad_scale_mlp = grad_hidden_two * normed_two
    grad_middle = upstream + norm_back(grad_hidden_two * (1.0 + scale_mlp), normed_two, inverse_two)
    grad_gate_attn = grad_middle * attention_projected
    grad_attn_proj = (grad_middle * gate_attn).astype(jnp.bfloat16)
    grad_out = jnp.einsum("td,te->de", attn_low, grad_attn_proj, preferred_element_type=jnp.float32)
    grad_attended = jnp.einsum(
        "te,de->td", grad_attn_proj, out_back, preferred_element_type=jnp.float32
    )
    grad_heads = grad_attended.astype(jnp.bfloat16).reshape(tok_rows, heads, HD)
    delta_rows = jnp.sum(grad_heads.astype(jnp.float32) * attn_rows, axis=-1)
    query_delta = jnp.transpose(delta_rows)
    lse_rows = jnp.transpose(query_lse)
    lse_high = lse_rows.astype(jnp.bfloat16)
    lse_rest = (lse_rows - lse_high.astype(jnp.float32)).astype(jnp.bfloat16)
    delta_high = delta_rows.astype(jnp.bfloat16)
    delta_rest = (delta_rows - delta_high.astype(jnp.float32)).astype(jnp.bfloat16)
    stat_rows = jnp.concatenate([lse_high, lse_rest, delta_high, delta_rest], axis=1)
    zero_heads = jnp.zeros((tok_rows, heads, HD), jnp.float32)
    partial_value = (zero_heads, zero_heads, zero_heads)
    grad_query = partial_value[0]
    key_rows = lax.all_gather(key_own, "ctx", axis=0, tiled=True)

    def query_visit(partial_value, scan_item):
        key_part, value_part, part_start = scan_item

        def query_update(partial_value):
            key_block = (part_start + jnp.arange(tok_rows, dtype=jnp.int32)) // BLOCK
            allowed = (key_block[None, :] <= query_block[:, None])[None]
            scores = (
                jnp.einsum("qhd,khd->hqk", queries, key_part, preferred_element_type=jnp.float32)
                * score_scale
            )
            probs = jnp.where(allowed, jnp.exp(scores - query_lse[..., None]), 0.0)
            grad_prob = jnp.einsum(
                "qhd,khd->hqk", grad_heads, value_part, preferred_element_type=jnp.float32
            )
            grad_score = (probs * (grad_prob - query_delta[..., None]) * score_scale).astype(
                jnp.bfloat16
            )
            return partial_value + jnp.einsum(
                "hqk,khd->qhd", grad_score, key_part, preferred_element_type=jnp.float32
            )

        return (
            lax.cond(
                part_start // BLOCK <= query_block[-1], query_update, keep_same, partial_value
            ),
            None,
        )

    grad_query, unused = lax.scan(
        query_visit,
        grad_query,
        (
            split_rows(key_rows, tok_rows),
            split_rows(lax.all_gather(value_own, "ctx", axis=0, tiled=True), tok_rows),
            part_starts(key_rows.shape[0], tok_rows),
        ),
    )
    key_partial_value = (partial_value[1], partial_value[2])
    query_rows = lax.all_gather(queries, "ctx", axis=0, tiled=True)

    def key_visit(running, scan_item):
        query_part, dout_part, stat_part, part_start = scan_item

        def key_update(running):
            grad_key, grad_value = running
            query_blk = (part_start + jnp.arange(tok_rows, dtype=jnp.int32)) // BLOCK
            allowed = (query_blk[:, None] >= query_block[None, :])[None]
            stat_float = stat_part.astype(jnp.float32)
            lse_part = jnp.transpose(stat_float[:, :heads] + stat_float[:, heads : 2 * heads])
            delta_part = jnp.transpose(
                stat_float[:, 2 * heads : 3 * heads] + stat_float[:, 3 * heads :]
            )
            scores = (
                jnp.einsum("qhd,khd->hqk", query_part, key_own, preferred_element_type=jnp.float32)
                * score_scale
            )
            probs = jnp.where(allowed, jnp.exp(scores - lse_part[..., None]), 0.0)
            grad_value = grad_value + jnp.einsum(
                "hqk,qhd->khd",
                probs.astype(jnp.bfloat16),
                dout_part,
                preferred_element_type=jnp.float32,
            )
            grad_prob = jnp.einsum(
                "qhd,khd->hqk", dout_part, value_own, preferred_element_type=jnp.float32
            )
            grad_score = (probs * (grad_prob - delta_part[..., None]) * score_scale).astype(
                jnp.bfloat16
            )
            grad_key = grad_key + jnp.einsum(
                "hqk,qhd->khd", grad_score, query_part, preferred_element_type=jnp.float32
            )
            return (grad_key, grad_value)

        last_seen = (part_start + tok_rows - 1) // BLOCK
        return (lax.cond(last_seen >= query_block[0], key_update, keep_same, running), None)

    key_partial_value, unused = lax.scan(
        key_visit,
        key_partial_value,
        (
            split_rows(query_rows, tok_rows),
            split_rows(lax.all_gather(grad_heads, "ctx", axis=0, tiled=True), tok_rows),
            split_rows(lax.all_gather(stat_rows, "ctx", axis=0, tiled=True), tok_rows),
            part_starts(query_rows.shape[0], tok_rows),
        ),
    )
    grad_key, grad_value = key_partial_value
    grad_query, grad_key, grad_value = (grad_query, grad_key, grad_value)
    grad_query = rotate_back(grad_query, cosine_table, sine_table)
    grad_key = rotate_back(grad_key, cosine_table, sine_table)
    grad_projected = (
        jnp.stack([grad_query, grad_key, grad_value], axis=1)
        .reshape(tok_rows, 3 * model_width)
        .astype(jnp.bfloat16)
    )
    grad_qkv = jnp.einsum(
        "td,te->de", residual_first, grad_projected, preferred_element_type=jnp.float32
    )
    grad_hidden_one = jnp.einsum(
        "te,de->td", grad_projected, qkv_back, preferred_element_type=jnp.float32
    )
    grad_scale_attn = grad_hidden_one * normed_one
    input_grad = grad_middle + norm_back(
        grad_hidden_one * (1.0 + scale_attn), normed_one, inverse_one
    )
    grad_modulation = jnp.concatenate(
        [grad_scale_attn, grad_gate_attn, grad_scale_mlp, grad_gate_mlp], axis=1
    )
    grad_blocks = jnp.sum(
        grad_modulation.reshape(tok_rows // BLOCK, BLOCK, 4 * model_width), axis=1
    )
    embedded_float = embedded.astype(jnp.float32)
    halves = (
        lax.psum_scatter(
            grad_qkv.astype(jnp.bfloat16), "fsdp", scatter_dimension=0, tiled=True
        ).astype(jnp.float32),
        lax.psum_scatter(
            grad_out.astype(jnp.bfloat16), "fsdp", scatter_dimension=0, tiled=True
        ).astype(jnp.float32),
        lax.psum_scatter(
            grad_up.astype(jnp.bfloat16), "fsdp", scatter_dimension=0, tiled=True
        ).astype(jnp.float32),
        lax.psum_scatter(
            grad_down.astype(jnp.bfloat16), "fsdp", scatter_dimension=0, tiled=True
        ).astype(jnp.float32),
    )
    totals = lax.psum((halves[0], halves[1], halves[2], halves[3]), "ctx")
    all_embedded, all_blocks = (
        lax.all_gather(embedded_float, ("ctx", "fsdp"), axis=0, tiled=True),
        lax.all_gather(grad_blocks, ("ctx", "fsdp"), axis=0, tiled=True),
    )
    shard_width = model_width // lax.axis_size("fsdp")
    row_start = lax.axis_index("fsdp") * shard_width
    embedded_part = lax.dynamic_slice_in_dim(all_embedded, row_start, shard_width, 1)
    ada_total = jnp.dot(jnp.transpose(embedded_part), all_blocks, precision=highest_precision)
    return (result[None], input_grad[None], totals[0], totals[1], totals[2], totals[3], ada_total)


def solution(mesh):
    return jax.shard_map(
        on_device,
        mesh=mesh,
        in_specs=(
            P("fsdp", "ctx", None),
            P("fsdp", "ctx"),
            P(),
            P("fsdp", None),
            P("fsdp", None),
            P("fsdp", None),
            P("fsdp", None),
            P("fsdp", None),
            P("fsdp", "ctx", None),
        ),
        out_specs=(
            P("fsdp", "ctx", None),
            P("fsdp", "ctx", None),
            P("fsdp", None),
            P("fsdp", None),
            P("fsdp", None),
            P("fsdp", None),
            P("fsdp", None),
        ),
        check_vma=False,
    )
```

profile of v0, /device:TPU:1, one launch (start us, length us, event | category | flops | bytes accessed | tf_op | source)
XLA Modules:
  0.0 1367.9 jit_solution(16312369276463341289)
XLA Ops:
  11.8 49.2 %all-gather.16.cloned.1.call-done = bf16[768,2304]{1,0:T(8,128)(2,1)} async-done(((bf16[384,2304]{1,0:T(8,128)(2,1)}), bf16[768,2304]{1,0:T(8,128)(2,1)}) %all-gather.16.cloned.1.call-update) | async-done | bytes 3538960 | tf_op jit(solution)/shard_map/all_gather | solution.py:121
  66.8 58.5 %all-gather.14.cloned.1.call-done = bf16[768,3072]{1,0:T(8,128)(2,1)} async-done(((bf16[384,3072]{1,0:T(8,128)(2,1)}), bf16[768,3072]{1,0:T(8,128)(2,1)}) %all-gather.14.cloned.1.call-update) | async-done | bytes 4718608 | tf_op jit(solution)/shard_map/all_gather | solution.py:125
  136.7 61.5 %all-gather.18.cloned.1.call-done = bf16[4096,12,64]{0,2,1:T(8,128)(2,1)} async-done(((bf16[256,12,64]{0,2,1:T(8,128)(2,1)}), bf16[4096,12,64]{0,2,1:T(8,128)(2,1)}) %all-gather.18.cloned.1.call-update) | async-done | bytes 6291472 | tf_op jit(solution)/shard_map/all_gather | solution.py:155
  204.6 60.1 %all-gather.30.cloned.1.call-done = bf16[4096,1,12,64]{0,3,2,1:T(8,128)(2,1)} async-done(((bf16[256,1,12,64]{0,3,2,1:T(8,128)(2,1)}), bf16[4096,1,12,64]{0,3,2,1:T(8,128)(2,1)}) %all-gather.30.cloned.1.call-update) | async-done | bytes 6291472 | tf_op jit(solution)/shard_map/all_gather | solution.py:156
  275.7 105.9 %while.48 = (s32[]{:T(128)}, f32[12,256]{1,0:T(8,128)S(1)}, f32[12,256]{1,0:T(8,128)S(1)}, f32[12,256,64]{1,2,0:T(8,128)}, s32[16]{0:T(128)}, /*index=5*/s32[256...) while((s32[]{:T(128)}, f32[12,256]{1,0:T(8,128)S(1)}, ...), condition=%wide.region_7.8_spmd, body=%wide.region_2.7_spmd.sunk | while | flops 212019216 | bytes 18944504 | solution.py:102
  393.6 21.4 %all-gather.24.cloned.1.call-done = bf16[3072,768]{1,0:T(8,128)(2,1)} async-done(((bf16[1536,768]{1,0:T(8,128)(2,1)}), bf16[3072,768]{1,0:T(8,128)(2,1)}) %all-gather.24.cloned.1.call-update) | async-done | bytes 4718608 | tf_op jit(solution)/shard_map/all_gather | solution.py:124
  453.6 90.9 %all_gather.50 = bf16[4096,48]{0,1:T(8,128)(2,1)S(1)} all-gather(bf16[256,48]{0,1:T(8,128)(2,1)S(1)} %pad_maximum_fusion.2), channel_id=1, replica_groups=mesh['ctx'=16,'fsdp'=2] {'ctx'}, dimensions={0}, use_global_device_ids=true | all-gather | bytes 417792 | tf_op jit(solution)/shard_map/all_gather | solution.py:293
  552.7 105.8 %while.49 = (s32[]{:T(128)}, f32[256,12,64]{0,2,1:T(8,128)}, s32[16]{0:T(128)}, s32[256]{0:T(256)}, bf16[16,256,12,64]{1,3,2,0:T(8,128)(2,1)}, /*index=5*/bf16[2...) while((s32[]{:T(128)}, f32[256,12,64]{0,2,1:T(8,128)}, ...), condition=%wide.region_16.17_spmd, body=%wide.region_13.16_spmd.sunk | while | flops 307761184 | bytes 9995169 | solution.py:238
  666.8 237.7 %while.50 = (s32[]{:T(128)}, f32[256,12,64]{0,2,1:T(8,128)}, f32[256,12,64]{0,2,1:T(8,128)}, s32[16]{0:T(128)}, s32[256]{0:T(256)}, /*index=5*/bf16[16,256,12,64...) while((s32[]{:T(128)}, f32[256,12,64]{0,2,1:T(8,128)}, ...), condition=%wide.region_20.21_spmd, body=%wide.region_17.20_spmd.sunk | while | flops 411785248 | bytes 15332817 | solution.py:287
  689.9 11.9 conditional.8
  705.6 11.9 conditional.8
  721.2 11.9 conditional.8
  736.8 11.9 conditional.8
  752.4 11.9 conditional.8
  768.0 11.9 conditional.8
  783.6 11.9 conditional.8
  799.1 11.9 conditional.8
  814.7 11.9 conditional.8
  830.3 11.9 conditional.8
  845.9 11.9 conditional.8
  892.7 11.9 conditional.8
  913.3 67.8 %all-gather.3 = f32[32,1,768]{2,1,0:T(1,128)S(1)} all-gather(f32[1,1,768]{2,1,0:T(1,128)S(1)} %reshape.336), channel_id=3, replica_groups=mesh['ctx'=16,'fsdp'=2] {'ctx','fsdp'}, dimensions={0}, use_global_device_ids=true | all-gather | bytes 101376 | tf_op jit(solution)/shard_map/all_gather | solution.py:339
  987.2 66.9 %all-gather.2 = f32[98304]{0:T(1024)S(1)} all-gather(f32[3072]{0:T(1024)S(1)} %maximum_reduce_fusion), channel_id=4, replica_groups=mesh['ctx'=16,'fsdp'=2] {'ctx','fsdp'}, dimensions={0}, use_global_device_ids=true | all-gather | bytes 405504 | tf_op jit(solution)/shard_map/all_gather | solution.py:340
  1060.6 300.3 %all-reduce.2 = (f32[384,2304]{1,0:T(8,128)}, f32[384,768]{1,0:T(8,128)}, f32[384,3072]{1,0:T(8,128)}, f32[1536,768]{1,0:T(8,128)}) all-reduce(bf16[384,2304]{1,0:T(8,128)(2,1)} %reduce-scatter.5.cloned.1.call-done, bf16[384,768]{1,0:T(8,128)(2,1)} %reduce-scatter.7.cloned.1.call-done, ...), channel_id=1, replica_groups=mesh['ctx'=16,'fsdp'=2] {'ctx'}, use_global_device_ids=true, to_apply=%region_24.25 | all-reduce | flops 3538944 | bytes 21233664 | tf_op jit(solution)/shard_map/psum | solution.py:337
  (459 shorter events, 515.4 us)
Async XLA Ops:
  7.2 53.9 %all-gather.16.cloned.1.call-start = ((), (), s32[]{:S(2)}) async-start(), calls=%async_computation.5 | async-start | bytes 5308416 | tf_op jit(solution)/shard_map/all_gather | solution.py:121
  7.9 117.3 %all-gather.14.cloned.1.call-start = ((), (), s32[]{:S(2)}) async-start(), calls=%async_computation.4 | async-start | bytes 7077888 | tf_op jit(solution)/shard_map/all_gather | solution.py:125
  8.7 189.6 %all-gather.18.cloned.1.call-start = ((), (), s32[]{:S(2)}) async-start(), calls=%async_computation.6 | async-start | bytes 6684672 | tf_op jit(solution)/shard_map/all_gather | solution.py:155
  11.4 119.3 %copy-start.21 = (f32[256,64]{0,1:T(8,128)}, f32[256,64]{0,1:T(8,128)S(1)}, u32[]{:S(2)}) copy-start(f32[256,64]{0,1:T(8,128)S(1)} %get-tuple-element.968) | copy-start | bytes 196612
  11.4 119.3 %copy-start.23 = (f32[256,64]{0,1:T(8,128)}, f32[256,64]{0,1:T(8,128)S(1)}, u32[]{:S(2)}) copy-start(f32[256,64]{0,1:T(8,128)S(1)} %get-tuple-element.969) | copy-start | bytes 196612
  11.6 117.5 %copy-start.28 = (f32[256]{0:T(256)}, f32[256]{0:T(256)S(1)}, u32[]{:S(2)}) copy-start(f32[256]{0:T(256)S(1)} %broadcast_multiply_fusion.7) | copy-start | bytes 3076
  11.8 117.3 %copy-start.30 = (f32[256]{0:T(256)}, f32[256]{0:T(256)S(1)}, u32[]{:S(2)}) copy-start(f32[256]{0:T(256)S(1)} %add_rsqrt_fusion.1) | copy-start | bytes 3076
  132.0 132.7 %all-gather.30.cloned.1.call-start = ((), (), s32[]{:S(2)}) async-start(), calls=%async_computation.16 | async-start | bytes 6684672 | tf_op jit(solution)/shard_map/all_gather | solution.py:156
  132.9 250.6 %all-gather.20.cloned.1.call-start = ((), (), s32[]{:S(2)}) async-start(), calls=%async_computation.7 | async-start | bytes 1769472 | tf_op jit(solution)/shard_map/all_gather | solution.py:122
  133.5 254.4 %all-gather.22.cloned.1.call-start = ((), (), s32[]{:S(2)}) async-start(), calls=%async_computation.8 | async-start | bytes 7077888 | tf_op jit(solution)/shard_map/all_gather | solution.py:123
  134.1 280.9 %all-gather.24.cloned.1.call-start = ((), (), s32[]{:S(2)}) async-start(), calls=%async_computation.9 | async-start | bytes 7077888 | tf_op jit(solution)/shard_map/all_gather | solution.py:124
  134.8 410.5 %all-gather.26.cloned.1.call-start = ((), (), s32[]{:S(2)}) async-start(), calls=%async_computation.10 | async-start | bytes 6684672 | tf_op jit(solution)/shard_map/all_gather | solution.py:248
  135.6 523.0 %all-gather.28.cloned.1.call-start = ((), (), s32[]{:S(2)}) async-start(), calls=%async_computation.11 | async-start | bytes 6684672 | tf_op jit(solution)/shard_map/all_gather | solution.py:292
  275.6 107.8 %copy-start.6 = (bf16[1,256,768]{2,1,0:T(8,128)(2,1)S(1)}, bf16[1,256,768]{2,1,0:T(8,128)(2,1)}, u32[]{:S(2)}) copy-start(bf16[1,256,768]{2,1,0:T(8,128)(2,1)} %param.21) | copy-start | bytes 1179652
  383.4 10.2 copy-start.14
  386.5 34.7 %copy-start.35 = (f32[256]{0:T(256)}, f32[256]{0:T(256)S(1)}, u32[]{:S(2)}) copy-start(f32[256]{0:T(256)S(1)} %broadcast_multiply_fusion.6) | copy-start | bytes 3076
  387.9 33.4 %copy-start.36 = (f32[256]{0:T(256)}, f32[256]{0:T(256)S(1)}, u32[]{:S(2)}) copy-start(f32[256]{0:T(256)S(1)} %add_rsqrt_fusion) | copy-start | bytes 3076
  387.9 27.1 %copy-start.37 = (f32[768]{0:T(1024)S(1)}, f32[768]{0:T(1024)}, u32[]{:S(2)}) copy-start(f32[768]{0:T(1024)} %get-tuple-element.957) | copy-start | bytes 9220
  415.0 9.8 copy-start.44
  432.8 548.9 %reduce-scatter.7.cloned.1.call-start = ((), (), s32[]{:S(2)}) async-start(), calls=%async_computation.13 | async-start | bytes 1769472 | tf_op jit(solution)/shard_map/reduce_scatter | solution.py:327
  435.4 546.4 %reduce-scatter.9.cloned.1.call-start = ((), (), s32[]{:S(2)}) async-start(), calls=%async_computation.14 | async-start | bytes 7077888 | tf_op jit(solution)/shard_map/reduce_scatter | solution.py:330
  441.0 540.7 %reduce-scatter.11.cloned.1.call-start = ((), (), s32[]{:S(2)}) async-start(), calls=%async_computation.15 | async-start | bytes 7077888 | tf_op jit(solution)/shard_map/reduce_scatter | solution.py:333
  448.4 612.2 %reduce-scatter.5.cloned.1.call-start = ((), (), s32[]{:S(2)}) async-start(), calls=%async_computation.12 | async-start | bytes 5308416 | tf_op jit(solution)/shard_map/reduce_scatter | solution.py:324
  1054.1 306.8 %copy-start.1 = (f32[1024,768]{1,0:T(8,128)S(1)}, f32[1024,768]{1,0:T(8,128)}, u32[]{:S(2)}) copy-start(f32[1024,768]{1,0:T(8,128)} %param.23) | copy-start | bytes 9437188
  (36 other events, 111.8 us)
Sparse Core Ops, SparseCore 0:
  9.6 51.4 all-gather.15
  62.6 62.6 all-gather.13
  132.1 66.0 all-gather.17
  200.8 63.8 all-gather.29
  266.1 20.5 all-gather.19
  288.1 62.6 all-gather.21
  352.3 62.6 all-gather.23
  417.2 66.0 all-gather.25
  485.4 86.1 all-gather.27
  574.3 19.7 reduce-scatter.6
  597.1 59.9 reduce-scatter.8
  659.9 60.0 reduce-scatter.10
  912.7 50.0 reduce-scatter.4
where the time goes:
time: 1390 us; the launch traced here: 1370 us
  blocking collectives  526 us (38%)
  waiting for transfers between devices  255 us (18%)
  matrix products  203 us (15%)
  local copies, waits for them, and re-layouts  168 us (12%)
  loops' own time  125 us (9%)
  other arithmetic  74.6 us (5%)
  between operations  15.7 us (1%)
    psum x1, blocking collectives, on_device(): totals = lax.psum((halves[0], halves[1], halves[2], halves[3]), 'ctx')  300 us
    all_gather x1, blocking collectives, on_device(): lax.all_gather(stat_rows, 'ctx', axis=0, tiled=True)  90.9 us
    all_gather x1, blocking collectives, on_device(): lax.all_gather(embedded_float, ('ctx', 'fsdp'), axis=0, tiled=True)  67.8 us
    all_gather x1, blocking collectives, on_device(): lax.all_gather(grad_blocks, ('ctx', 'fsdp'), axis=0, tiled=True)  66.9 us
    dynamic_slice x48, local copies, waits for them, and re-layouts, attend_forward(): lax.scan(attend_visit, partial_value, (split_rows(key_rows, sub_rows), sp...  62.2 us
    all_gather x1, waiting for transfers between devices, on_device(): lax.all_gather(key_own, 'ctx', axis=0, tiled=True)  61.5 us
    all_gather x1, waiting for transfers between devices, on_device(): lax.all_gather(value_own, 'ctx', axis=0, tiled=True)  60.1 us
    dot_general x15, matrix products, key_update(): jnp.einsum('hqk,qhd->khd', grad_score, query_part, preferred_element_type...  59.2 us
  transfers between devices with their start and end apart: 13, of which 5 were waited for; matrix products, arithmetic and copies ran while one was open for 32% of the time, Pallas kernels for 0%

commit v1 on v0

--- a/solution.py
+++ b/solution.py
@@ -1,12 +1,17 @@
+import functools
 import math
 
 import jax
 import jax.numpy as jnp
 from jax import lax
+from jax.experimental import pallas as pl
+from jax.experimental.pallas import tpu as pltpu
 from jax.sharding import PartitionSpec as P
 
 HD = 64
 BLOCK = 256
+VMEM_LIMIT = 60 * 1024 * 1024
+MESH = pl.DeviceIdType.MESH
 
 
 norm_eps = 1e-06
@@ -346,9 +351,785 @@
     return (result[None], input_grad[None], totals[0], totals[1], totals[2], totals[3], ada_total)
 
 
+def barrier_with(peers):
+    barrier = pltpu.get_barrier_semaphore()
+    for peer in peers:
+        pl.semaphore_signal(barrier, inc=1, device_id=peer, device_id_type=MESH)
+    pl.semaphore_wait(barrier, len(peers))
+
+
+def plane_barrier(me, count):
+    barrier = pltpu.get_barrier_semaphore()
+
+    def greet(step, carry):
+        pl.semaphore_signal(
+            barrier,
+            inc=1,
+            device_id={"ctx": lax.rem(me + step, count)},
+            device_id_type=MESH,
+        )
+        return carry
+
+    lax.fori_loop(1, count, greet, 0)
+    pl.semaphore_wait(barrier, count - 1)
+
+
+def remote(source, target, send_sem, recv_sem, **where):
+    return pltpu.make_async_remote_copy(
+        src_ref=source,
+        dst_ref=target,
+        send_sem=send_sem,
+        recv_sem=recv_sem,
+        device_id=where,
+        device_id_type=MESH,
+    )
+
+
+def landed(ref, sem):
+    pltpu.make_async_copy(ref, ref, sem).wait()
+
+
+def gather_kernel(
+    emb_ref, ada_ref, qkv_ref, out_ref, up_ref, down_ref,
+    mod_ref, qkv_full, out_full, up_full, down_full,
+    emb_other, part_other, part_send,
+    own_sem, small_send, small_recv, send_sem, recv_sem,
+):
+    me = lax.axis_index("ctx")
+    row = lax.axis_index("fsdp")
+    other = 1 - row
+    piece = lax.rem(me, 4)
+    chip_next = jnp.bitwise_xor(me, 2)
+    sibling = jnp.bitwise_xor(me, 1)
+    barrier_with([{"fsdp": other}, {"ctx": chip_next}, {"ctx": sibling}])
+    emb_copy = remote(emb_ref, emb_other, small_send.at[0], small_recv.at[0], fsdp=other)
+    emb_copy.start()
+    shards = (qkv_ref, out_ref, up_ref, down_ref)
+    wholes = (qkv_full, out_full, up_full, down_full)
+    started = []
+    for index in range(4):
+        shard, whole = shards[index], wholes[index]
+        half = shard.shape[0]
+        part = half // 4
+        copy = remote(
+            shard.at[pl.ds(piece * part, part)],
+            whole.at[pl.ds(row * half + piece * part, part)],
+            send_sem.at[index, 0], recv_sem.at[index, 0], fsdp=other,
+        )
+        copy.start()
+        started.append(copy)
+    for index in range(4):
+        shard, whole = shards[index], wholes[index]
+        half = shard.shape[0]
+        pltpu.make_async_copy(
+            shard, whole.at[pl.ds(row * half, half)], own_sem.at[index]
+        ).start()
+    emb_copy.wait()
+    half_width = ada_ref.shape[0]
+    cols = pl.ds(pl.multiple_of(row * half_width, 128), half_width)
+    both = jnp.concatenate([emb_ref[:, cols], emb_other[:, cols]], axis=0).astype(jnp.bfloat16)
+    partial = jnp.dot(both, ada_ref[...], preferred_element_type=jnp.float32)
+    mod_ref[...] = partial[:8]
+    part_send[...] = partial[8:]
+    part_copy = remote(part_send, part_other, small_send.at[1], small_recv.at[1], fsdp=other)
+    part_copy.start()
+
+    def rows_of(index, which):
+        half = shards[index].shape[0]
+        part = half // 4
+        return wholes[index].at[pl.ds(other * half + which * part, part)]
+
+    def pass_on(index):
+        landed(rows_of(index, piece), recv_sem.at[index, 0])
+        for slot, peer in ((1, chip_next), (2, sibling)):
+            copy = remote(
+                rows_of(index, piece), rows_of(index, piece),
+                send_sem.at[index, slot], recv_sem.at[index, slot], ctx=peer,
+            )
+            copy.start()
+            started.append(copy)
+
+    def pass_last(index):
+        across = jnp.bitwise_xor(piece, 2)
+        landed(rows_of(index, across), recv_sem.at[index, 1])
+        copy = remote(
+            rows_of(index, across), rows_of(index, across),
+            send_sem.at[index, 3], recv_sem.at[index, 3], ctx=sibling,
+        )
+        copy.start()
+        started.append(copy)
+
+    for index in range(4):
+        pass_on(index)
+        if index:
+            pass_last(index - 1)
+    pass_last(3)
+    part_copy.wait()
+    mod_ref[...] += part_other[...]
+    for index in range(4):
+        landed(rows_of(index, jnp.bitwise_xor(piece, 1)), recv_sem.at[index, 2])
+        landed(rows_of(index, jnp.bitwise_xor(piece, 3)), recv_sem.at[index, 3])
+        half = shards[index].shape[0]
+        pltpu.make_async_copy(
+            shards[index], wholes[index].at[pl.ds(row * half, half)], own_sem.at[index]
+        ).wait()
+    for copy in started:
+        copy.wait_send()
+
+
+def gather_weights(embedded, w_ada, w_qkv, w_out, w_up, w_down):
+    shards = (w_qkv, w_out, w_up, w_down)
+    width = w_ada.shape[1]
+    emb_rows = jnp.broadcast_to(embedded.astype(jnp.float32), (8, embedded.shape[1]))
+    hbm = pl.BlockSpec(memory_space=pl.ANY)
+    vmem = pl.BlockSpec(memory_space=pltpu.VMEM)
+    return pl.pallas_call(
+        gather_kernel,
+        out_shape=[jax.ShapeDtypeStruct((8, width), jnp.float32)]
+        + [jax.ShapeDtypeStruct((2 * w.shape[0], w.shape[1]), w.dtype) for w in shards],
+        in_specs=[vmem, vmem] + [hbm] * 4,
+        out_specs=[vmem] + [hbm] * 4,
+        scratch_shapes=[
+            pltpu.VMEM(emb_rows.shape, jnp.float32),
+            pltpu.VMEM((8, width), jnp.float32),
+            pltpu.VMEM((8, width), jnp.float32),
+            pltpu.SemaphoreType.DMA((4,)),
+            pltpu.SemaphoreType.DMA((2,)),
+            pltpu.SemaphoreType.DMA((2,)),
+            pltpu.SemaphoreType.DMA((4, 4)),
+            pltpu.SemaphoreType.DMA((4, 4)),
+        ],
+        compiler_params=pltpu.CompilerParams(
+            collective_id=1, has_side_effects=True, vmem_limit_bytes=VMEM_LIMIT
+        ),
+    )(emb_rows, w_ada, *shards)
+
+
+def head_place(me):
+    plane = me // 4
+    spot = lax.rem(me, 4)
+    odd = lax.rem(plane, 2)
+    idle = 3 - 2 * odd
+    head = 3 * plane + spot - odd * (spot // 2)
+    return spot != idle, head
+
+
+def head_owner(head):
+    plane = head // 3
+    rank = lax.rem(head, 3)
+    odd = lax.rem(plane, 2)
+    return 4 * plane + rank + odd * ((rank + 1) // 2)
+
+
+def scatter_heads(me, heads, source, target, send_sem, recv_sem):
+    def send(step, carry):
+        head = lax.rem(step + 3 * (me // 4), heads)
+        owner = head_owner(head)
+
+        @pl.when(owner != me)
+        def _():
+            remote(
+                source.at[head], target.at[me], send_sem.at[head], recv_sem.at[me], ctx=owner
+            ).start()
+
+        @pl.when(owner == me)
+        def _():
+            pltpu.make_async_copy(source.at[head], target.at[me], recv_sem.at[me]).start()
+
+        return carry
+
+    lax.fori_loop(0, heads, send, 0)
+
+
+def scatter_sent(me, heads, source, target, send_sem, recv_sem):
+    def finish(head, carry):
+        owner = head_owner(head)
+
+        @pl.when(owner != me)
+        def _():
+            remote(
+                source.at[head], target.at[me], send_sem.at[head], recv_sem.at[me], ctx=owner
+            ).wait_send()
+
+        return carry
+
+    lax.fori_loop(0, heads, finish, 0)
+
+
+def return_block(me, head, block, source, target, send_sem, recv_sem):
+    @pl.when(block != me)
+    def _():
+        remote(
+            source.at[block], target.at[head], send_sem.at[block], recv_sem.at[head], ctx=block
+        ).start()
+
+    @pl.when(block == me)
+    def _():
+        pltpu.make_async_copy(source.at[block], target.at[head], recv_sem.at[head]).start()
+
+
+def return_sent(me, head, blocks, source, target, send_sem, recv_sem):
+    def finish(block, carry):
+        @pl.when(block != me)
+        def _():
+            remote(
+                source.at[block], target.at[head], send_sem.at[block], recv_sem.at[head], ctx=block
+            ).wait_send()
+
+        return carry
+
+    lax.fori_loop(0, blocks, finish, 0)
+
+
+def wait_heads(heads, target, recv_sem):
+    def finish(head, carry):
+        landed(target.at[head], recv_sem.at[head])
+        return carry
+
+    lax.fori_loop(0, heads, finish, 0)
+
+
+def transposed(values):
+    return jnp.transpose(values.astype(jnp.float32)).astype(values.dtype)
+
+
+def forward_kernel(
+    blocks, heads, qkv_ref, att_ref, buf_ref, out_ref, lse_ref,
+    pair_ref, low_ref, send_sem, recv_sem, back_send, back_recv,
+):
+    me = lax.axis_index("ctx")
+    owner, head = head_place(me)
+    plane_barrier(me, blocks)
+    scatter_heads(me, heads, qkv_ref, buf_ref, send_sem, recv_sem)
+
+    @pl.when(owner)
+    def _():
+        def query_block(block, carry):
+            landed(buf_ref.at[block], recv_sem.at[block])
+            rows = pl.ds(pl.multiple_of(block * BLOCK, BLOCK), BLOCK)
+            pair_ref[rows, :] = transposed(buf_ref[block, HD:, :])
+            query = jnp.concatenate(
+                [buf_ref[block, :HD, :], jnp.zeros((HD, BLOCK), jnp.bfloat16)], axis=0
+            )
+
+            def key_block(key, state):
+                high, total, mixed = state
+                key_rows = pl.ds(pl.multiple_of(key * BLOCK, BLOCK), BLOCK)
+                scores = jnp.dot(pair_ref[key_rows, :], query, preferred_element_type=jnp.float32)
+                new_high = jnp.maximum(high, jnp.max(scores, axis=0, keepdims=True))
+                weights = jnp.exp(scores - new_high)
+                decay = jnp.exp(high - new_high)
+                total = total * decay + jnp.sum(weights, axis=0, keepdims=True)
+                mixed = mixed * decay + jnp.dot(
+                    buf_ref[key, 2 * HD :, :],
+                    weights.astype(jnp.bfloat16),
+                    preferred_element_type=jnp.float32,
+                )
+                return new_high, total, mixed
+
+            high, total, mixed = lax.fori_loop(
+                0,
+                block + 1,
+                key_block,
+                (
+                    jnp.full((1, BLOCK), masked_score, jnp.float32),
+                    jnp.zeros((1, BLOCK), jnp.float32),
+                    jnp.zeros((HD, BLOCK), jnp.float32),
+                ),
+            )
+            mixed = mixed / total
+            out_ref[block] = mixed
+            low_ref[block] = mixed.astype(jnp.bfloat16)
+            lse_ref[block] = jnp.broadcast_to(high + jnp.log(total), (8, BLOCK))
+            return_block(me, head, block, low_ref, att_ref, back_send, back_recv)
+            return carry
+
+        lax.fori_loop(0, blocks, query_block, 0)
+        return_sent(me, head, blocks, low_ref, att_ref, back_send, back_recv)
+
+    scatter_sent(me, heads, qkv_ref, buf_ref, send_sem, recv_sem)
+    wait_heads(heads, att_ref, back_recv)
+
+
+def attention_forward(qkv_heads, blocks):
+    heads = qkv_heads.shape[0]
+    vmem = pl.BlockSpec(memory_space=pltpu.VMEM)
+    return pl.pallas_call(
+        functools.partial(forward_kernel, blocks, heads),
+        out_shape=[
+            jax.ShapeDtypeStruct((heads, HD, BLOCK), jnp.bfloat16),
+            jax.ShapeDtypeStruct((blocks, 3 * HD, BLOCK), jnp.bfloat16),
+            jax.ShapeDtypeStruct((blocks, HD, BLOCK), jnp.float32),
+            jax.ShapeDtypeStruct((blocks, 8, BLOCK), jnp.float32),
+        ],
+        in_specs=[vmem],
+        out_specs=[vmem] * 4,
+        scratch_shapes=[
+            pltpu.VMEM((blocks * BLOCK, 2 * HD), jnp.bfloat16),
+            pltpu.VMEM((blocks, HD, BLOCK), jnp.bfloat16),
+            pltpu.SemaphoreType.DMA((heads,)),
+            pltpu.SemaphoreType.DMA((blocks,)),
+            pltpu.SemaphoreType.DMA((blocks,)),
+            pltpu.SemaphoreType.DMA((heads,)),
+        ],
+        compiler_params=pltpu.CompilerParams(
+            collective_id=2, has_side_effects=True, vmem_limit_bytes=VMEM_LIMIT
+        ),
+    )(qkv_heads)
+
+
+def backward_kernel(
+    blocks, heads, dout_ref, buf_ref, out_ref, lse_ref, grad_ref,
+    got_ref, pair_ref, total_ref, low_ref, send_sem, recv_sem, back_send, back_recv,
+):
+    me = lax.axis_index("ctx")
+    owner, head = head_place(me)
+    plane_barrier(me, blocks)
+    scatter_heads(me, heads, dout_ref, got_ref, send_sem, recv_sem)
+
+    @pl.when(owner)
+    def _():
+        def prepare(block, carry):
+            rows = pl.ds(pl.multiple_of(block * BLOCK, BLOCK), BLOCK)
+            pair_ref[rows, :] = transposed(buf_ref[block, HD:, :])
+            total_ref[rows, :] = jnp.zeros((BLOCK, 2 * HD), jnp.float32)
+            return carry
+
+        lax.fori_loop(0, blocks, prepare, 0)
+
+        def query_block(step, carry):
+            block = blocks - 1 - step
+            landed(got_ref.at[block], recv_sem.at[block])
+            dout = got_ref[block]
+            query = buf_ref[block, :HD, :]
+            zero = jnp.zeros((HD, BLOCK), jnp.bfloat16)
+            delta = jnp.sum(dout.astype(jnp.float32) * out_ref[block], axis=0, keepdims=True)
+            lse = lse_ref[block, :1, :]
+            query_down = jnp.concatenate([query, zero], axis=0)
+            dout_down = jnp.concatenate([zero, dout], axis=0)
+            dout_side = transposed(jnp.concatenate([dout, zero], axis=0))
+            query_side = transposed(jnp.concatenate([zero, query], axis=0))
+
+            def key_block(key, grad_query):
+                key_rows = pl.ds(pl.multiple_of(key * BLOCK, BLOCK), BLOCK)
+                pair = pair_ref[key_rows, :]
+                scores = jnp.dot(pair, query_down, preferred_element_type=jnp.float32)
+                probs = jnp.exp(scores - lse)
+                grad_probs = jnp.dot(pair, dout_down, preferred_element_type=jnp.float32)
+                grad_scores = (probs * (grad_probs - delta)).astype(jnp.bfloat16)
+                total_ref[key_rows, :] += jnp.dot(
+                    probs.astype(jnp.bfloat16), dout_side, preferred_element_type=jnp.float32
+                ) + jnp.dot(grad_scores, query_side, preferred_element_type=jnp.float32)
+                return grad_query + jnp.dot(
+                    buf_ref[key, HD : 2 * HD, :], grad_scores, preferred_element_type=jnp.float32
+                )
+
+            grad_query = lax.fori_loop(
+                0, block + 1, key_block, jnp.zeros((HD, BLOCK), jnp.float32)
+            )
+            rows = pl.ds(pl.multiple_of(block * BLOCK, BLOCK), BLOCK)
+            low_ref[block, :HD, :] = (grad_query * (1.0 / math.sqrt(HD))).astype(jnp.bfloat16)
+            sums = jnp.transpose(total_ref[rows, :]).astype(jnp.bfloat16)
+            low_ref[block, HD : 2 * HD, :] = sums[HD:]
+            low_ref[block, 2 * HD :, :] = sums[:HD]
+            return_block(me, head, block, low_ref, grad_ref, back_send, back_recv)
+            return carry
+
+        lax.fori_loop(0, blocks, query_block, 0)
+        return_sent(me, head, blocks, low_ref, grad_ref, back_send, back_recv)
+
+    scatter_sent(me, heads, dout_ref, got_ref, send_sem, recv_sem)
+    wait_heads(heads, grad_ref, back_recv)
+
+
+def attention_backward(dout_heads, buffered, mixed, lse):
+    heads = dout_heads.shape[0]
+    blocks = buffered.shape[0]
+    vmem = pl.BlockSpec(memory_space=pltpu.VMEM)
+    return pl.pallas_call(
+        functools.partial(backward_kernel, blocks, heads),
+        out_shape=jax.ShapeDtypeStruct((heads, 3 * HD, BLOCK), jnp.bfloat16),
+        in_specs=[vmem] * 4,
+        out_specs=vmem,
+        scratch_shapes=[
+            pltpu.VMEM((blocks, HD, BLOCK), jnp.bfloat16),
+            pltpu.VMEM((blocks * BLOCK, 2 * HD), jnp.bfloat16),
+            pltpu.VMEM((blocks * BLOCK, 2 * HD), jnp.float32),
+            pltpu.VMEM((blocks, 3 * HD, BLOCK), jnp.bfloat16),
+            pltpu.SemaphoreType.DMA((heads,)),
+            pltpu.SemaphoreType.DMA((blocks,)),
+            pltpu.SemaphoreType.DMA((blocks,)),
+            pltpu.SemaphoreType.DMA((heads,)),
+        ],
+        compiler_params=pltpu.CompilerParams(
+            collective_id=3, has_side_effects=True, vmem_limit_bytes=VMEM_LIMIT
+        ),
+    )(dout_heads, buffered, mixed, lse)
+
+
+def reduce_kernel(
+    units, planes, part_ref, stat_ref, res_ref, table_ref,
+    sib_ref, row_ref, x_ref, z_ref,
+    s_sib, r_sib, s_row, r_row, s_x, r_x, s_z, r_z, s_az, r_az, s_ax, r_ax, s_as, r_as,
+    s_t, r_t,
+):
+    me = lax.axis_index("ctx")
+    row = lax.axis_index("fsdp")
+    other = 1 - row
+    core = lax.rem(me, 2)
+    xbit = lax.rem(me // 2, 2)
+    plane = me // 4
+    spot = lax.rem(me, 4)
+    sibling = jnp.bitwise_xor(me, 1)
+    chip_next = jnp.bitwise_xor(me, 2)
+    barrier = pltpu.get_barrier_semaphore()
+    peers = [{"fsdp": other}, {"ctx": sibling}, {"ctx": chip_next}]
+    peers += [{"ctx": lax.rem(me + 4 * step, 4 * planes)} for step in range(1, planes)]
+    for peer in peers:
+        pl.semaphore_signal(barrier, inc=1, device_id=peer, device_id_type=MESH)
+    pl.semaphore_wait(barrier, len(peers))
+    width = part_ref.shape[3] // 2
+    mine = pl.ds(pl.multiple_of(core * width, 128), width)
+    theirs = pl.ds(pl.multiple_of((1 - core) * width, 128), width)
+    deep = part_ref.shape[2]
+    quarter = deep // 2
+    small = quarter // planes
+
+    def add(left, right):
+        return (left.astype(jnp.float32) + right.astype(jnp.float32)).astype(jnp.bfloat16)
+
+    def to_sibling(unit):
+        return [
+            remote(part_ref.at[unit, half, :, theirs], sib_ref.at[unit, half],
+                   s_sib.at[unit, half], r_sib.at[unit, half], ctx=sibling)
+            for half in range(2)
+        ]
+
+    def to_row(unit):
+        return [remote(sib_ref.at[unit, other], row_ref.at[unit],
+                       s_row.at[unit], r_row.at[unit], fsdp=other)]
+
+    def to_x(unit):
+        rows = pl.ds(pl.multiple_of((1 - xbit) * quarter, 16), quarter)
+        return [remote(row_ref.at[unit, rows], x_ref.at[unit],
+                       s_x.at[unit], r_x.at[unit], ctx=chip_next)]
+
+    def to_z(unit):
+        copies = []
+        for step in range(1, planes):
+            goal = lax.rem(plane + step, planes)
+            rows = pl.ds(pl.multiple_of(goal * small, 16), small)
+            copies.append(
+                remote(x_ref.at[unit, rows], z_ref.at[unit, step - 1],
+                       s_z.at[unit, step - 1], r_z.at[unit, step - 1], ctx=4 * goal + spot)
+            )
+        return copies
+
+    def piece(unit, which):
+        rows = pl.ds(pl.multiple_of(xbit * quarter + which * small, 16), small)
+        return res_ref.at[unit, rows, mine]
+
+    def along_z(unit):
+        return [
+            remote(piece(unit, plane), piece(unit, plane),
+                   s_az.at[unit, step - 1], r_az.at[unit, step - 1],
+                   ctx=4 * lax.rem(plane + step, planes) + spot)
+            for step in range(1, planes)
+        ]
+
+    def along_x(unit):
+        rows = pl.ds(pl.multiple_of(xbit * quarter, 16), quarter)
+        ref = res_ref.at[unit, rows, mine]
+        return [remote(ref, ref, s_ax.at[unit], r_ax.at[unit], ctx=chip_next)]
+
+    def along_s(unit):
+        ref = res_ref.at[unit, :, mine]
+        return [remote(ref, ref, s_as.at[unit], r_as.at[unit], ctx=sibling)]
+
+    def launch(copies):
+        for copy in copies:
+            copy.start()
+
+    def stage0(unit):
+        launch(to_sibling(unit))
+
+    def stage1(unit):
+        for half in range(2):
+            landed(sib_ref.at[unit, half], r_sib.at[unit, half])
+            sib_ref[unit, half] = add(sib_ref[unit, half], part_ref[unit, half, :, mine])
+        launch(to_row(unit))
+
+    def stage2(unit):
+        landed(row_ref.at[unit], r_row.at[unit])
+        row_ref[unit] = add(row_ref[unit], sib_ref[unit, row])
+        launch(to_x(unit))
+
+    def stage3(unit):
+        landed(x_ref.at[unit], r_x.at[unit])
+        rows = pl.ds(pl.multiple_of(xbit * quarter, 16), quarter)
+        x_ref[unit] = add(x_ref[unit], row_ref[unit, rows])
+        launch(to_z(unit))
+
+    def stage4(unit):
+        rows = pl.ds(pl.multiple_of(plane * small, 16), small)
+        total = x_ref[unit, rows].astype(jnp.float32)
+        for step in range(1, planes):
+            landed(z_ref.at[unit, step - 1], r_z.at[unit, step - 1])
+            total += z_ref[unit, step - 1].astype(jnp.float32)
+        spots = pl.ds(pl.multiple_of(xbit * quarter + plane * small, 16), small)
+        res_ref[unit, spots, mine] = total.astype(jnp.bfloat16)
+        launch(along_z(unit))
+
+    def stage5(unit):
+        for step in range(1, planes):
+            landed(piece(unit, lax.rem(plane + planes - step, planes)), r_az.at[unit, step - 1])
+        launch(along_x(unit))
+
+    def stage6(unit):
+        rows = pl.ds(pl.multiple_of((1 - xbit) * quarter, 16), quarter)
+        landed(res_ref.at[unit, rows, mine], r_ax.at[unit])
+        launch(along_s(unit))
+
+    def stage7(unit):
+        landed(res_ref.at[unit, :, theirs], r_as.at[unit])
+        for make in (to_sibling, to_row, to_x, to_z, along_z, along_x, along_s):
+            for copy in make(unit):
+                copy.wait_send()
+
+    stages = (stage0, stage1, stage2, stage3, stage4, stage5, stage6, stage7)
+
+    def slots(first, count):
+        return table_ref.at[pl.ds(first, count)]
+
+    chip_slot = core * 4 * planes + 4 * plane
+
+    def table_row():
+        return [remote(slots(chip_slot + 2 * xbit + row, 1), slots(chip_slot + 2 * xbit + row, 1),
+                       s_t.at[0], r_t.at[0], fsdp=other)]
+
+    def table_x():
+        return [remote(slots(chip_slot + 2 * xbit, 2), slots(chip_slot + 2 * xbit, 2),
+                       s_t.at[1], r_t.at[1], ctx=chip_next)]
+
+    def table_z():
+        return [remote(slots(chip_slot, 4), slots(chip_slot, 4), s_t.at[2 + step],
+                       r_t.at[2 + step], ctx=4 * lax.rem(plane + step, planes) + spot)
+                for step in range(1, planes)]
+
+    def table_s():
+        return [remote(slots(core * 4 * planes, 4 * planes), slots(core * 4 * planes, 4 * planes),
+                       s_t.at[2], r_t.at[2], ctx=sibling)]
+
+    table_ref[chip_slot + 2 * xbit + row] = stat_ref[...]
+    launch(table_row())
+
+    def tick(time, carry):
+        @pl.when(time == 1)
+        def _():
+            landed(slots(chip_slot + 2 * xbit + other, 1), r_t.at[0])
+            launch(table_x())
+
+        @pl.when(time == 3)
+        def _():
+            landed(slots(chip_slot + 2 * (1 - xbit), 2), r_t.at[1])
+            launch(table_z())
+
+        @pl.when(time == 5)
+        def _():
+            for step in range(1, planes):
+                goal = lax.rem(plane + planes - step, planes)
+                landed(slots(core * 4 * planes + 4 * goal, 4), r_t.at[2 + step])
+            launch(table_s())
+
+        for depth in range(len(stages)):
+            unit = time - depth
+
+            @pl.when((unit >= 0) & (unit < units))
+            def _(depth=depth, unit=unit):
+                stages[depth](unit)
+
+        return carry
+
+    lax.fori_loop(0, units + len(stages) - 1, tick, 0)
+    landed(slots((1 - core) * 4 * planes, 4 * planes), r_t.at[2])
+    for copies in (table_row(), table_x(), table_z(), table_s()):
+        for copy in copies:
+            copy.wait_send()
+
+
+def reduce_gradients(parts, stats, count):
+    units, halves, deep, width = parts.shape
+    planes = count // 4
+    vmem = pl.BlockSpec(memory_space=pltpu.VMEM)
+    dma = pltpu.SemaphoreType.DMA
+    steps = planes - 1
+    sems = [(units, 2), (units, 2), (units,), (units,), (units,), (units,),
+            (units, steps), (units, steps), (units, steps), (units, steps),
+            (units,), (units,), (units,), (units,), (planes + 2,), (planes + 2,)]
+    return pl.pallas_call(
+        functools.partial(reduce_kernel, units, planes),
+        out_shape=[
+            jax.ShapeDtypeStruct((units, deep, width), jnp.bfloat16),
+            jax.ShapeDtypeStruct((2 * count,) + stats.shape, jnp.float32),
+        ],
+        in_specs=[vmem, vmem],
+        out_specs=[vmem, vmem],
+        scratch_shapes=[
+            pltpu.VMEM((units, 2, deep, width // 2), jnp.bfloat16),
+            pltpu.VMEM((units, deep, width // 2), jnp.bfloat16),
+            pltpu.VMEM((units, deep // 2, width // 2), jnp.bfloat16),
+            pltpu.VMEM((units, steps, deep // 2 // planes, width // 2), jnp.bfloat16),
+        ] + [dma(shape) for shape in sems],
+        compiler_params=pltpu.CompilerParams(
+            collective_id=4, has_side_effects=True, vmem_limit_bytes=VMEM_LIMIT
+        ),
+    )(parts, stats)
+
+
+def to_units(gradient, model_width):
+    rows, cols = gradient.shape
+    low = gradient.astype(jnp.bfloat16)
+    if rows == model_width:
+        count = cols // model_width
+        return jnp.transpose(low.reshape(2, rows // 2, count, model_width), (2, 0, 1, 3))
+    count = rows // model_width
+    return jnp.transpose(low.reshape(2, count, model_width // 2, model_width), (1, 0, 2, 3))
+
+
+def from_units(summed, rows):
+    count, deep, width = summed.shape
+    values = summed.astype(jnp.float32)
+    if rows == deep:
+        return jnp.transpose(values, (1, 0, 2)).reshape(deep, count * width)
+    return values.reshape(count * deep, width)
+
+
+def fast_device(tokens, timestep, time_table, w_qkv, w_out, w_up, w_down, w_ada, cotangent):
+    tok_rows = tokens.shape[1]
+    model_width = tokens.shape[2]
+    heads = model_width // HD
+    blocks = lax.axis_size("ctx")
+    me = lax.axis_index("ctx")
+    score_scale = 1.0 / math.sqrt(HD)
+    embedded = lax.dynamic_slice_in_dim(time_table, timestep[0, 0], 1, 0).astype(jnp.bfloat16)
+    modulation, qkv_full, out_full, up_full, down_full = gather_weights(
+        embedded, w_ada, w_qkv, w_out, w_up, w_down
+    )
+    scale_attn, gate_attn, scale_mlp, gate_mlp = jnp.split(modulation[:1], 4, axis=1)
+    inputs = tokens[0].astype(jnp.float32)
+    normed_one, inverse_one = layer_norm(inputs)
+    residual_first = (normed_one * (1.0 + scale_attn)).astype(jnp.bfloat16)
+    projected = jnp.transpose(
+        jnp.dot(residual_first, qkv_full, preferred_element_type=jnp.float32)
+    ).reshape(3, heads, HD, tok_rows)
+    positions = me * tok_rows + jnp.arange(tok_rows, dtype=jnp.int32)
+    cosine_table, sine_table = rope_tables(positions, HD)
+    cosine = jnp.transpose(cosine_table[:, 0, :])
+    sine = jnp.transpose(sine_table[:, 0, :])
+
+    def turn(values):
+        return jnp.concatenate([-values[:, HD // 2 :], values[:, : HD // 2]], axis=1)
+
+    queries = projected[0] * cosine + turn(projected[0]) * sine
+    key_own = projected[1] * cosine + turn(projected[1]) * sine
+    qkv_heads = jnp.concatenate(
+        [
+            queries.astype(jnp.bfloat16) * jnp.bfloat16(score_scale),
+            key_own.astype(jnp.bfloat16),
+            projected[2].astype(jnp.bfloat16),
+        ],
+        axis=1,
+    )
+    att_heads, buffered, mixed, lse = attention_forward(qkv_heads, blocks)
+    attn_low = jnp.transpose(att_heads.reshape(model_width, tok_rows))
+    attention_projected = jnp.dot(attn_low, out_full, preferred_element_type=jnp.float32)
+    middle = inputs + gate_attn * attention_projected
+    normed_two, inverse_two = layer_norm(middle)
+    residual_second = (normed_two * (1.0 + scale_mlp)).astype(jnp.bfloat16)
+    before_activation = jnp.dot(residual_second, up_full, preferred_element_type=jnp.float32)
+    gelu_activated, gelu_back = jax.vjp(gelu_tanh, before_activation)
+    act_low = gelu_activated.astype(jnp.bfloat16)
+    feedforward_output = jnp.dot(act_low, down_full, preferred_element_type=jnp.float32)
+    result = middle + gate_mlp * feedforward_output
+    upstream = cotangent[0].astype(jnp.float32)
+    grad_gate_mlp = upstream * feedforward_output
+    grad_mlp = (upstream * gate_mlp).astype(jnp.bfloat16)
+    grad_down = jnp.einsum("tf,td->fd", act_low, grad_mlp, preferred_element_type=jnp.float32)
+    grad_act = jnp.einsum("td,fd->tf", grad_mlp, down_full, preferred_element_type=jnp.float32)
+    grad_pre = gelu_back(grad_act)[0].astype(jnp.bfloat16)
+    grad_up = jnp.einsum("td,tf->df", residual_second, grad_pre, preferred_element_type=jnp.float32)
+    grad_hidden_two = jnp.einsum("tf,df->td", grad_pre, up_full, preferred_element_type=jnp.float32)
+    grad_scale_mlp = grad_hidden_two * normed_two
+    grad_middle = upstream + norm_back(grad_hidden_two * (1.0 + scale_mlp), normed_two, inverse_two)
+    grad_gate_attn = grad_middle * attention_projected
+    grad_attn_proj = (grad_middle * gate_attn).astype(jnp.bfloat16)
+    grad_out = jnp.einsum("td,te->de", attn_low, grad_attn_proj, preferred_element_type=jnp.float32)
+    grad_attended = jnp.einsum(
+        "de,te->dt", out_full, grad_attn_proj, preferred_element_type=jnp.float32
+    )
+    dout_heads = grad_attended.astype(jnp.bfloat16).reshape(heads, HD, tok_rows)
+    grad_heads = attention_backward(dout_heads, buffered, mixed, lse)
+
+    def turn_back(values):
+        scaled = values * sine
+        return values * cosine - turn(scaled)
+
+    wide = grad_heads.astype(jnp.float32)
+    grad_projected = jnp.transpose(
+        jnp.stack(
+            [
+                turn_back(wide[:, :HD]),
+                turn_back(wide[:, HD : 2 * HD]),
+                wide[:, 2 * HD :],
+            ]
+        )
+        .reshape(3 * model_width, tok_rows)
+        .astype(jnp.bfloat16)
+    )
+    grad_qkv = jnp.einsum(
+        "td,te->de", residual_first, grad_projected, preferred_element_type=jnp.float32
+    )
+    grad_hidden_one = jnp.einsum(
+        "te,de->td", grad_projected, qkv_full, preferred_element_type=jnp.float32
+    )
+    grad_scale_attn = grad_hidden_one * normed_one
+    input_grad = grad_middle + norm_back(
+        grad_hidden_one * (1.0 + scale_attn), normed_one, inverse_one
+    )
+    grad_blocks = jnp.concatenate(
+        [
+            jnp.sum(values, axis=0, keepdims=True)
+            for values in (grad_scale_attn, grad_gate_attn, grad_scale_mlp, grad_gate_mlp)
+        ],
+        axis=1,
+    )
+    stats = jnp.concatenate([embedded.astype(jnp.float32), grad_blocks], axis=1).reshape(-1, 128)
+    stat_rows = stats.shape[0]
+    stats = jnp.pad(stats, ((0, -stat_rows % 8), (0, 0)))
+    gradients = (grad_qkv, grad_out, grad_up, grad_down)
+    grouped = [to_units(gradient, model_width) for gradient in gradients]
+    summed, table = reduce_gradients(jnp.concatenate(grouped), stats, blocks)
+    totals = []
+    first = 0
+    for group, shard in zip(grouped, (w_qkv, w_out, w_up, w_down)):
+        totals.append(from_units(summed[first : first + group.shape[0]], shard.shape[0]))
+        first += group.shape[0]
+    flat = table[:, :stat_rows].reshape(2 * blocks, 5 * model_width)
+    shard_width = model_width // 2
+    embedded_part = lax.dynamic_slice_in_dim(
+        flat[:, :model_width], lax.axis_index("fsdp") * shard_width, shard_width, 1
+    )
+    ada_total = lax.dot_general(
+        embedded_part, flat[:, model_width:], (((0,), (0,)), ((), ())),
+        precision=lax.Precision.HIGHEST,
+    )
+    return (result[None], input_grad[None], *totals, ada_total)
+
+
 def solution(mesh):
+    chosen = fast_device if mesh.shape["ctx"] == 16 else on_device
     return jax.shard_map(
-        on_device,
+        chosen,
         mesh=mesh,
         in_specs=(
             P("fsdp", "ctx", None),

time: 1390 us -> 621 us (0.45); the launches traced: 1370 us -> 620 us
  blocking collectives: 526 us -> 0 us
  Pallas kernels: 0 us -> 503 us
  waiting for transfers between devices: 255 us -> 0 us
  matrix products: 203 us -> 35.7 us
  loops' own time: 125 us -> 0 us
  local copies, waits for them, and re-layouts: 168 us -> 51.8 us
  other arithmetic: 74.6 us -> 28.2 us
    pallas_call x0 -> x4, Pallas kernels: none -> 503 us  [the longest x1 220 us: gather_weights(): pl.pallas_call(gather_kernel, out_shape=[jax.ShapeDtypeStruct((8, width),...]
    psum x1 -> x0, blocking collectives: 300 us -> none  [on_device(): totals = lax.psum((halves[0], halves[1], halves[2], halves[3]), 'ctx')]
    all_gather x9 -> x0, waiting for transfers between devices: 251 us -> none  [the longest x1 61.5 us: on_device(): lax.all_gather(key_own, 'ctx', axis=0, tiled=True)]
    all_gather x3 -> x0, blocking collectives: 226 us -> none  [the longest x1 90.9 us: on_device(): lax.all_gather(stat_rows, 'ctx', axis=0, tiled=True)]
    dot_general x68 -> x13, matrix products: 203 us -> 35.7 us  [the longest x1 5.51 us: fast_device(): lax.dot_general(embedded_part, flat[:, model_width:], (((0,), (0,)), ((),...]
    another operation x51 -> x0, loops' own time: 125 us -> none  [the longest x1 52.7 us: attend_forward(): lax.scan(attend_visit, partial_value, (split_rows(key_rows, sub_rows), sp...]
    dynamic_slice x49 -> x0, local copies, waits for them, and re-layouts: 62.8 us -> none  [the longest x48 62.2 us: attend_forward(): lax.scan(attend_visit, partial_value, (split_rows(key_rows, sub_rows), sp...]
    slice x49 -> x3, local copies, waits for them, and re-layouts: 57 us -> 0.79 us  [the longest x1 0.64 us: fast_device(): flat[:, :model_width]]
  transfers between devices with their start and end apart: 13 -> 0, of which waited for: 5 -> 0; matrix products, arithmetic and copies ran while one was open for 32% -> 0% of each run, Pallas kernels for 0% -> 0%
where the time goes in v1:
time: 621 us; the launch traced here: 620 us
  Pallas kernels  503 us (81%)
  local copies, waits for them, and re-layouts  51.8 us (8%)
  matrix products  35.7 us (6%)
  other arithmetic  28.2 us (5%)
    pallas_call x1, Pallas kernels, gather_weights(): pl.pallas_call(gather_kernel, out_shape=[jax.ShapeDtypeStruct((8, width),...  220 us
    pallas_call x1, Pallas kernels, reduce_gradients(): pl.pallas_call(functools.partial(reduce_kernel, units, planes), out_shape...  117 us
    pallas_call x1, Pallas kernels, attention_backward(): pl.pallas_call(functools.partial(backward_kernel, blocks, heads), out_sha...  86.8 us
    pallas_call x1, Pallas kernels, attention_forward(): pl.pallas_call(functools.partial(forward_kernel, blocks, heads), out_shap...  78.4 us
    reshape x4, local copies, waits for them, and re-layouts, to_units(): low.reshape(2, rows // 2, count, model_width)  23 us
    unnamed x64, local copies, waits for them, and re-layouts  14.9 us

profile of v1, /device:TPU:1, one launch (start us, length us, event | category | flops | bytes accessed | tf_op | source)
XLA Modules:
  0.0 620.3 jit_solution(6877152870026839346)
XLA Ops:
  5.3 220.4 %shard_map.144 = (f32[8,3072]{1,0:T(8,128)}, bf16[768,2304]{1,0:T(8,128)(2,1)}, bf16[768,768]{1,0:T(8,128)(2,1)}, bf16[768,3072]{1,0:T(8,128)(2,1)}, bf16[3072,768]{1,0:T(8,128)(2,1)}) custom-call(f32[8,768]{1,0:T(8,128)} %broadcast_in_dim.17.emb_ref, bf16[384,3072]{1,0:T(8,128)(2,1)} %ada_ref.1, bf16[384,2304]{1,0:T(8,128)(2,1)} %qkv_ref.1, ...), custom_call_target="tpu_custom_call" | custom-call | tf_op jit(solution)/shard_map/pallas_call | solution.py:486
  226.5 3.2 fusion.37
  231.5 78.4 %shard_map.145 = (bf16[12,64,256]{2,1,0:T(8,128)(2,1)}, bf16[16,192,256]{2,1,0:T(8,128)(2,1)}, f32[16,64,256]{2,1,0:T(8,128)}, f32[16,8,256]{2,1,0:T(8,128)}) custom-call(bf16[12,192,256]{2,1,0:T(8,128)(2,1)} %pad_maximum_fusion.1.qkv_ref), custom_call_target="tpu_custom_call" | custom-call | tf_op jit(solution)/shard_map/pallas_call | solution.py:657
  311.8 4.2 fusion.54
  316.1 3.0 fusion.6
  320.9 3.2 fusion.27
  325.3 86.8 %shard_map.146 = bf16[12,192,256]{2,1,0:T(8,128)(2,1)} custom-call(bf16[12,64,256]{2,1,0:T(8,128)(2,1)} %bitcast.135, bf16[16,192,256]{2,1,0:T(8,128)(2,1)} %get-tuple-element.24.buf_ref, f32[16,64,256]{2,1,0:T(8,128)} %get-tuple-element.25.out_ref, f32[16,8,256]{2,1,0:T(8,128)} %get-tuple-element.26.lse_ref), custom_call_target="tpu_custom_call" | custom-call | tf_op jit(solution)/shard_map/pallas_call | solution.py:749
  419.9 4.2 convolution_convert_fusion
  424.1 2.5 copy.31
  427.9 5.3 reshape.169
  433.3 4.8 copy.33
  438.1 3.7 convolution_convert_fusion.1
  441.8 9.8 %reshape.149 = bf16[2,384,4,768]{3,2,1,0:T(4,128)(2,1)} reshape(bf16[768,3072]{1,0:T(8,128)(2,1)} %convolution_convert_fusion.1) | data formatting | bytes 9437184 | tf_op jit(solution)/shard_map/reshape | solution.py:994
  451.6 3.1 copy.32
  456.6 6.4 %pad_maximum_fusion.part_ref = bf16[12,2,384,768]{3,2,1,0:T(8,128)(2,1)} fusion(bf16[4,2,384,768]{3,2,1,0:T(8,128)(2,1)S(1)} %bitcast.118, bf16[4,2,384,768]{3,2,1,0:T(8,128)(2,1)S(1)} %bitcast.119, bf16[1,2,384,768]{3,2,1,0:T(8,128)(2,1)S(1)} %bitcast.127, bf16[3,2,384,768]{3,2,1,0:T(8,128)(2,1)S(1)} %bitcast.122), kind=kLoop, calls=%fused_computation | loop fusion | flops 21233664 | bytes 28311552 | tf_op jit(solution)/shard_map/concatenate | solution.py:1111
  463.0 117.2 %shard_map.147 = (bf16[12,384,768]{2,1,0:T(8,128)(2,1)}, f32[32,32,128]{2,1,0:T(8,128)}) custom-call(bf16[12,2,384,768]{3,2,1,0:T(8,128)(2,1)} %pad_maximum_fusion.part_ref, f32[32,128]{1,0:T(8,128)} %pad.4.stat_ref), custom_call_target="tpu_custom_call" | custom-call | tf_op jit(solution)/shard_map/pallas_call | solution.py:969
  585.1 3.6 convert_bitcast_fusion.1
  588.6 3.3 copy.20
  591.9 2.9 copy.22
  594.9 5.1 fusion.58
  600.0 2.7 bitcast_convert_fusion
  602.7 5.5 fusion.39
  608.2 6.1 copy.21
  614.3 6.0 copy.23
  (108 shorter events, 27.0 us)
Async XLA Ops:
  5.3 221.2 %copy-start = (bf16[1,256,768]{2,1,0:T(8,128)(2,1)S(1)}, bf16[1,256,768]{2,1,0:T(8,128)(2,1)}, u32[]{:S(2)}) copy-start(bf16[1,256,768]{2,1,0:T(8,128)(2,1)} %param.9) | copy-start | bytes 1179652
  230.2 79.7 %copy-start.7 = (bf16[768,768]{1,0:T(8,128)(2,1)S(1)}, bf16[768,768]{1,0:T(8,128)(2,1)}, u32[]{:S(2)}) copy-start(bf16[768,768]{1,0:T(8,128)(2,1)} %get-tuple-element.21) | copy-start | bytes 3538948
  311.5 9.3 %copy-start.3 = (f32[256,768]{1,0:T(8,128)}, f32[256,768]{1,0:T(8,128)S(1)}, u32[]{:S(2)}) copy-start(f32[256,768]{1,0:T(8,128)S(1)} %get-tuple-element.49) | copy-start | bytes 2359300
  311.5 9.3 %copy-start.17 = (f32[256]{0:T(256)}, f32[256]{0:T(256)S(1)}, u32[]{:S(2)}) copy-start(f32[256]{0:T(256)S(1)} %broadcast_multiply_fusion.4) | copy-start | bytes 3076
  311.5 4.5 slice-start.2
  311.8 9.1 %copy-start.19 = (f32[256]{0:T(256)}, f32[256]{0:T(256)S(1)}, u32[]{:S(2)}) copy-start(f32[256]{0:T(256)S(1)} %add_rsqrt_fusion) | copy-start | bytes 3076
  311.8 4.3 slice-start.3
  311.8 4.3 copy-start.21
  311.8 7.3 %slice-start.4 = ((s8[4718592]{0:T(1024)(128)(4,1)}), s8[4194304]{0:T(1024)(128)(4,1)S(1)}, s32[]{:S(2)}) async-start(s8[4718592]{0:T(1024)(128)(4,1)} %bitcast.141), calls=%async_computation.4 | async-start | bytes 8388608
  316.1 4.8 copy-start.22
  316.1 3.0 slice-start.5
  324.1 88.1 %copy-start.13 = (bf16[12,64,256]{2,1,0:T(8,128)(2,1)S(1)}, bf16[12,64,256]{2,1,0:T(8,128)(2,1)}, u32[]{:S(2)}) copy-start(bf16[12,64,256]{2,1,0:T(8,128)(2,1)} %get-tuple-element.20) | copy-start | bytes 1179652
  414.8 3.2 copy-start.8
  424.1 2.6 copy-start.1
  433.3 4.8 copy-start.4
  433.3 4.8 copy-start.15
  433.3 4.8 copy-start.18
  433.3 4.8 copy-start.20
  441.8 12.9 %slice-start = ((s8[4718592]{0:T(1024)(128)(4,1)}), s8[524288]{0:T(1024)(128)(4,1)S(1)}, s32[]{:S(2)}) async-start(s8[4718592]{0:T(1024)(128)(4,1)} %bitcast.116), calls=%async_computation | async-start | bytes 1048576
  451.6 3.6 slice-start.1
  451.6 4.7 copy-start.2
  451.6 5.0 copy-start.6
  600.0 2.7 copy-start.12
  600.0 2.7 copy-start.16
  (5 other events, 9.0 us)

commit v2 on v0

--- a/solution.py
+++ b/solution.py
@@ -1,12 +1,18 @@
+import functools
 import math
 
 import jax
 import jax.numpy as jnp
+import numpy as np
 from jax import lax
+from jax.experimental import pallas as pl
+from jax.experimental.pallas import tpu as pltpu
 from jax.sharding import PartitionSpec as P
 
 HD = 64
 BLOCK = 256
+VMEM_LIMIT = 62 * 1024 * 1024
+MESH = pl.DeviceIdType.MESH
 
 
 norm_eps = 1e-06
@@ -346,9 +352,954 @@
     return (result[None], input_grad[None], totals[0], totals[1], totals[2], totals[3], ada_total)
 
 
+def remote(source, target, send_sem, recv_sem, **where):
+    return pltpu.make_async_remote_copy(
+        src_ref=source,
+        dst_ref=target,
+        send_sem=send_sem,
+        recv_sem=recv_sem,
+        device_id=where,
+        device_id_type=MESH,
+    )
+
+
+def landed(ref, sem):
+    pltpu.make_async_copy(ref, ref, sem).wait()
+
+
+def head_place(me):
+    plane = me // 4
+    spot = lax.rem(me, 4)
+    odd = lax.rem(plane, 2)
+    idle = 3 - 2 * odd
+    head = 3 * plane + spot - odd * (spot // 2)
+    return spot != idle, head
+
+
+def head_owner(head):
+    plane = head // 3
+    rank = lax.rem(head, 3)
+    odd = lax.rem(plane, 2)
+    return 4 * plane + rank + odd * ((rank + 1) // 2)
+
+
+def scatter_sent(me, heads, source, target, send_sem, recv_sem):
+    def finish(head, carry):
+        owner = head_owner(head)
+
+        @pl.when(owner != me)
+        def _():
+            remote(
+                source.at[head], target.at[me], send_sem.at[head], recv_sem.at[me], ctx=owner
+            ).wait_send()
+
+        return carry
+
+    lax.fori_loop(0, heads, finish, 0)
+
+
+def return_block(me, head, block, source, target, send_sem, recv_sem):
+    @pl.when(block != me)
+    def _():
+        remote(
+            source.at[block], target.at[head], send_sem.at[block], recv_sem.at[head], ctx=block
+        ).start()
+
+    @pl.when(block == me)
+    def _():
+        pltpu.make_async_copy(source.at[block], target.at[head], recv_sem.at[head]).start()
+
+
+def return_sent(me, head, blocks, source, target, send_sem, recv_sem):
+    def finish(block, carry):
+        @pl.when(block != me)
+        def _():
+            remote(
+                source.at[block], target.at[head], send_sem.at[block], recv_sem.at[head], ctx=block
+            ).wait_send()
+
+        return carry
+
+    lax.fori_loop(0, blocks, finish, 0)
+
+
+def wait_heads(heads, target, recv_sem):
+    def finish(head, carry):
+        landed(target.at[head], recv_sem.at[head])
+        return carry
+
+    lax.fori_loop(0, heads, finish, 0)
+
+
+def transposed(values):
+    return jnp.transpose(values.astype(jnp.float32)).astype(values.dtype)
+
+
+def add_into(target, left, right, rows):
+    step = 48
+
+    def body(index, carry):
+        spot = pl.ds(pl.multiple_of(index * step, step), step)
+        total = left(spot).astype(jnp.float32) + right(spot).astype(jnp.float32)
+        target(spot, total.astype(jnp.bfloat16))
+        return carry
+
+    lax.fori_loop(0, rows // step, body, 0)
+
+
+def product(left, right):
+    return jnp.dot(left, right, preferred_element_type=jnp.float32)
+
+
+def product_back(left, right):
+    return lax.dot_general(
+        left, right, (((1,), (1,)), ((), ())), preferred_element_type=jnp.float32
+    )
+
+
+def layer_kernel(
+    blocks, heads,
+    tok_ref, cot_ref, emb_ref, rope_ref, ada_hbm, qkv_hbm, out_hbm, up_hbm, down_hbm,
+    result_ref, ingrad_ref, table_ref, og_qkv, og_out, og_up, og_down,
+    wq, wo, wu, wd, mod_ref, emb_other, part_other, part_send,
+    hid1_t, mid_ref, ap_ref, sums_ref, cos_ref, sin_ref,
+    qs_ref, buf_ref, mix_ref, lse_ref, att_ref, douts_ref, got_ref,
+    parts, sib_ref, row_ref, x_ref, z_ref, res_ref, stage_ref,
+    own_sem, small_send, small_recv, w_send, w_recv,
+    fs, fr, fbs, fbr, bs, br, bbs, bbr,
+    s_sib, r_sib, s_row, r_row, s_x, r_x, s_z, r_z, s_az, r_az, s_ax, r_ax, s_as, r_as,
+    s_t, r_t, out_sem, free_sem,
+):
+    me = lax.axis_index("ctx")
+    row = lax.axis_index("fsdp")
+    other = 1 - row
+    piece = lax.rem(me, 4)
+    core = lax.rem(me, 2)
+    xbit = lax.rem(me // 2, 2)
+    plane = me // 4
+    planes = blocks // 4
+    chip_next = jnp.bitwise_xor(me, 2)
+    sibling = jnp.bitwise_xor(me, 1)
+    gland_ref = qs_ref
+    owner, head = head_place(me)
+    width = tok_ref.shape[1]
+    score_scale = 1.0 / math.sqrt(HD)
+
+    barrier = pltpu.get_barrier_semaphore()
+    pl.semaphore_signal(barrier, inc=1, device_id={"fsdp": other}, device_id_type=MESH)
+
+    def greet(step, carry):
+        pl.semaphore_signal(
+            barrier, inc=1, device_id={"ctx": lax.rem(me + step, blocks)}, device_id_type=MESH
+        )
+        return carry
+
+    lax.fori_loop(1, blocks, greet, 0)
+    pl.semaphore_wait(barrier, blocks)
+
+    shards = (qkv_hbm, out_hbm, up_hbm, down_hbm)
+    wholes = (wq, wo, wu, wd)
+    quarter_rows = [shard.shape[0] // 4 for shard in shards]
+    chunks = [
+        (0, 0, quarter_rows[0] // 2),
+        (0, quarter_rows[0] // 2, quarter_rows[0] // 2),
+        (1, 0, quarter_rows[1]),
+        (2, 0, quarter_rows[2]),
+        (3, 0, quarter_rows[3]),
+    ]
+
+    def chunk_ref(index, which):
+        weight, first, count = chunks[index]
+        start = other * 4 * quarter_rows[weight] + which * quarter_rows[weight] + first
+        return wholes[weight].at[pl.ds(pl.multiple_of(start, 16), count)]
+
+    def y_copy(index):
+        weight, first, count = chunks[index]
+        near = piece * quarter_rows[weight] + first
+        far = row * 4 * quarter_rows[weight] + near
+        return remote(
+            shards[weight].at[pl.ds(pl.multiple_of(near, 16), count)],
+            wholes[weight].at[pl.ds(pl.multiple_of(far, 16), count)],
+            w_send.at[index, 0], w_recv.at[index, 0], fsdp=other,
+        )
+
+    def onward(index, which, slot, peer):
+        ref = chunk_ref(index, which)
+        return remote(ref, ref, w_send.at[index, slot], w_recv.at[index, slot], ctx=peer)
+
+    def pass_on(index):
+        landed(chunk_ref(index, piece), w_recv.at[index, 0])
+        onward(index, piece, 1, chip_next).start()
+        onward(index, piece, 2, sibling).start()
+
+    def pass_last(index):
+        across = jnp.bitwise_xor(piece, 2)
+        landed(chunk_ref(index, across), w_recv.at[index, 1])
+        onward(index, across, 3, sibling).start()
+
+    def chunk_done(index):
+        landed(chunk_ref(index, jnp.bitwise_xor(piece, 1)), w_recv.at[index, 2])
+        landed(chunk_ref(index, jnp.bitwise_xor(piece, 3)), w_recv.at[index, 3])
+
+    def own_copy(weight):
+        half = shards[weight].shape[0]
+        start = pl.multiple_of(row * half, 16)
+        return pltpu.make_async_copy(
+            shards[weight], wholes[weight].at[pl.ds(start, half)], own_sem.at[weight]
+        )
+
+    emb_copy = remote(emb_ref, emb_other, small_send.at[0], small_recv.at[0], fsdp=other)
+    emb_copy.start()
+    y_copy(0).start()
+    y_copy(1).start()
+
+    def opening(ada_ref, hid1):
+        ada_copy = pltpu.make_async_copy(ada_hbm, ada_ref, own_sem.at[4])
+        ada_copy.start()
+        for weight in range(4):
+            own_copy(weight).start()
+        half_width = width // 2
+        cols = pl.ds(pl.multiple_of(row * half_width, 128), half_width)
+        ada_copy.wait()
+        emb_copy.wait()
+        both = jnp.concatenate([emb_ref[:, cols], emb_other[:, cols]], axis=0)
+        partial = product(both.astype(jnp.bfloat16), ada_ref[...])
+        mod_ref[...] = partial[:8]
+        part_send[...] = partial[8:]
+        part_copy = remote(part_send, part_other, small_send.at[1], small_recv.at[1], fsdp=other)
+        part_copy.start()
+        lanes = lax.broadcasted_iota(jnp.int32, (HD // 2, 128), 1)
+        pick = lanes == me
+        cos_block = jnp.sum(jnp.where(pick, rope_ref[:, 2 * BLOCK : 2 * BLOCK + 128], 0.0), axis=1, keepdims=True)
+        sin_block = jnp.sum(jnp.where(pick, rope_ref[:, 2 * BLOCK + 128 :], 0.0), axis=1, keepdims=True)
+        cos_row = rope_ref[:, :BLOCK]
+        sin_row = rope_ref[:, BLOCK : 2 * BLOCK]
+        cos_ref[...] = cos_row * cos_block - sin_row * sin_block
+        sin_ref[...] = sin_row * cos_block + cos_row * sin_block
+        pass_on(0)
+        normed, unused = layer_norm(tok_ref[...].astype(jnp.float32))
+        part_copy.wait()
+        mod_ref[...] += part_other[...]
+        low = (normed * (1.0 + mod_ref[:1, :width])).astype(jnp.bfloat16)
+        hid1[...] = low
+        hid1_t[...] = transposed(low)
+        pass_on(1)
+        pass_last(0)
+        pass_last(1)
+        for index in (0, 1):
+            y_copy(index).wait_send()
+        for index in (2, 3, 4):
+            y_copy(index).start()
+        own_copy(0).wait()
+        chunk_done(0)
+        chunk_done(1)
+
+        def project(group, carry):
+            spans = []
+            for kind in range(3):
+                cols = pl.ds(pl.multiple_of(kind * width + group * 4 * HD, 4 * HD), 4 * HD)
+                spans.append(jnp.transpose(product(hid1[...], wq[:, cols])))
+            cos, sin = cos_ref[...], sin_ref[...]
+            for inner in range(4):
+                which = group * 4 + inner
+                for kind in range(2):
+                    top = spans[kind][inner * HD : inner * HD + HD // 2]
+                    low_half = spans[kind][inner * HD + HD // 2 : (inner + 1) * HD]
+                    turned = jnp.concatenate(
+                        [top * cos - low_half * sin, low_half * cos + top * sin], axis=0
+                    ).astype(jnp.bfloat16)
+                    if kind == 0:
+                        turned = turned * jnp.bfloat16(score_scale)
+                    qs_ref[which, kind * HD : (kind + 1) * HD, :] = turned
+                qs_ref[which, 2 * HD :, :] = spans[2][inner * HD : (inner + 1) * HD].astype(
+                    jnp.bfloat16
+                )
+                send_head(which, qs_ref, buf_ref, fs, fr)
+            return carry
+
+        lax.fori_loop(0, heads // 4, project, 0)
+
+    def send_head(which, source, target, send_sem, recv_sem):
+        goal = head_owner(which)
+
+        @pl.when(goal != me)
+        def _():
+            remote(
+                source.at[which], target.at[me], send_sem.at[which], recv_sem.at[me], ctx=goal
+            ).start()
+
+        @pl.when(goal == me)
+        def _():
+            pltpu.make_async_copy(source.at[which], target.at[me], recv_sem.at[me]).start()
+
+    pl.run_scoped(
+        opening,
+        pltpu.VMEM((width // 2, 4 * width), jnp.bfloat16),
+        pltpu.VMEM((BLOCK, width), jnp.bfloat16),
+    )
+
+    def forward(pair_ref, low_ref):
+        def attend(block):
+            landed(buf_ref.at[block], fr.at[block])
+            rows = pl.ds(pl.multiple_of(block * BLOCK, BLOCK), BLOCK)
+            pair_ref[rows, :] = transposed(buf_ref[block, HD:, :])
+            query = jnp.concatenate(
+                [buf_ref[block, :HD, :], jnp.zeros((HD, BLOCK), jnp.bfloat16)], axis=0
+            )
+
+            def key_block(key, state):
+                high, total, mixed = state
+                key_rows = pl.ds(pl.multiple_of(key * BLOCK, BLOCK), BLOCK)
+                scores = product(pair_ref[key_rows, :], query)
+                new_high = jnp.maximum(high, jnp.max(scores, axis=0, keepdims=True))
+                weights = jnp.exp(scores - new_high)
+                decay = jnp.exp(high - new_high)
+                total = total * decay + jnp.sum(weights, axis=0, keepdims=True)
+                mixed = mixed * decay + product(
+                    buf_ref[key, 2 * HD :, :], weights.astype(jnp.bfloat16)
+                )
+                return new_high, total, mixed
+
+            high, total, mixed = lax.fori_loop(
+                0,
+                block + 1,
+                key_block,
+                (
+                    jnp.full((1, BLOCK), masked_score, jnp.float32),
+                    jnp.zeros((1, BLOCK), jnp.float32),
+                    jnp.zeros((HD, BLOCK), jnp.float32),
+                ),
+            )
+            mixed = mixed / total
+            mix_ref[block] = mixed
+            low_ref[block] = mixed.astype(jnp.bfloat16)
+            lse_ref[block] = jnp.broadcast_to(high + jnp.log(total), (8, BLOCK))
+            return_block(me, head, block, low_ref, att_ref, fbs, fbr)
+
+        def visit(block, carry):
+            @pl.when(owner)
+            def _():
+                attend(block)
+
+            for when, event in FORWARD_EVENTS:
+                @pl.when(block == when)
+                def _(event=event):
+                    (pass_on, pass_last)[event[0]](event[1])
+
+            return carry
+
+        lax.fori_loop(0, blocks, visit, 0)
+
+        @pl.when(owner)
+        def _():
+            return_sent(me, head, blocks, low_ref, att_ref, fbs, fbr)
+
+        scatter_sent(me, heads, qs_ref, buf_ref, fs, fr)
+        wait_heads(heads, att_ref, fbr)
+
+    pl.run_scoped(
+        forward,
+        pltpu.VMEM((blocks * BLOCK, 2 * HD), jnp.bfloat16),
+        pltpu.VMEM((blocks, HD, BLOCK), jnp.bfloat16),
+    )
+
+    span = width // 2
+    mine = pl.ds(pl.multiple_of(core * span, 128), span)
+    theirs = pl.ds(pl.multiple_of((1 - core) * span, 128), span)
+    deep = width // 2
+    half_deep = deep // 2
+    small = half_deep // planes
+
+    def part_of(unit, half, cols):
+        return parts.at[unit, half, :, cols]
+
+    def qkv_part(unit, half, cols):
+        return wd.at[pl.ds(pl.multiple_of(((unit - 9) * 2 + half) * deep, 16), deep), cols]
+
+    def sib_of(unit, half):
+        return sib_ref.at[unit, half]
+
+    def qkv_sib(unit, half):
+        cols = pl.ds(pl.multiple_of(((unit - 9) * 2 + half) * span, 128), span)
+        return wu.at[pl.ds(0, deep), cols]
+
+    def pipeline(part, sib):
+        def to_sibling(unit):
+            return [
+                remote(part(unit, half, theirs), sib(unit, half),
+                       s_sib.at[unit, half], r_sib.at[unit, half], ctx=sibling)
+                for half in range(2)
+            ]
+
+        def to_row(unit):
+            return [remote(sib(unit, other), row_ref.at[unit],
+                           s_row.at[unit], r_row.at[unit], fsdp=other)]
+
+        def to_x(unit):
+            rows = pl.ds(pl.multiple_of((1 - xbit) * half_deep, 16), half_deep)
+            return [remote(row_ref.at[unit, rows], x_ref.at[unit],
+                           s_x.at[unit], r_x.at[unit], ctx=chip_next)]
+
+        def to_z(unit):
+            copies = []
+            for step in range(1, planes):
+                goal = lax.rem(plane + step, planes)
+                rows = pl.ds(pl.multiple_of(goal * small, 16), small)
+                copies.append(
+                    remote(x_ref.at[unit, rows], z_ref.at[unit, step - 1],
+                           s_z.at[unit, step - 1], r_z.at[unit, step - 1], ctx=4 * goal + piece)
+                )
+            return copies
+
+        def slab(unit, which):
+            rows = pl.ds(pl.multiple_of(xbit * half_deep + which * small, 16), small)
+            return res_ref.at[unit, rows, mine]
+
+        def along_z(unit):
+            return [
+                remote(slab(unit, plane), slab(unit, plane),
+                       s_az.at[unit, step - 1], r_az.at[unit, step - 1],
+                       ctx=4 * lax.rem(plane + step, planes) + piece)
+                for step in range(1, planes)
+            ]
+
+        def along_x(unit):
+            rows = pl.ds(pl.multiple_of(xbit * half_deep, 16), half_deep)
+            ref = res_ref.at[unit, rows, mine]
+            return [remote(ref, ref, s_ax.at[unit], r_ax.at[unit], ctx=chip_next)]
+
+        def along_s(unit):
+            ref = res_ref.at[unit, :, mine]
+            return [remote(ref, ref, s_as.at[unit], r_as.at[unit], ctx=sibling)]
+
+        def launch(copies):
+            for copy in copies:
+                copy.start()
+
+        def write_out(unit, which, cols):
+            def saved():
+                return pltpu.make_async_copy(
+                    stage_ref.at[which], og_out.at[:, pl.ds(0, span)], out_sem.at[which]
+                )
+
+            @pl.when(unit > 0)
+            def _():
+                saved().wait()
+
+            def convert(index, carry):
+                spot = pl.ds(pl.multiple_of(index * 48, 48), 48)
+                stage_ref[which, spot, :] = res_ref[unit, spot, cols].astype(jnp.float32)
+                return carry
+
+            lax.fori_loop(0, deep // 48, convert, 0)
+            side = core if which == 0 else 1 - core
+            kind = lax.rem(unit, 4)
+            order = 2 * (unit // 4) + lax.rem(kind, 2)
+
+            def save(target):
+                pltpu.make_async_copy(stage_ref.at[which], target, out_sem.at[which]).start()
+
+            @pl.when((unit < 8) & (kind < 2))
+            def _():
+                save(og_down.at[pl.ds(pl.multiple_of(order * deep, 8), deep),
+                                pl.ds(pl.multiple_of(side * span, 128), span)])
+
+            @pl.when((unit < 8) & (kind >= 2))
+            def _():
+                start = side * 4 * span + order * span
+                save(og_up.at[:, pl.ds(pl.multiple_of(start, 128), span)])
+
+            @pl.when(unit == 8)
+            def _():
+                save(og_out.at[:, pl.ds(pl.multiple_of(side * span, 128), span)])
+
+            @pl.when(unit > 8)
+            def _():
+                start = (unit - 9) * width + side * span
+                save(og_qkv.at[:, pl.ds(pl.multiple_of(start, 128), span)])
+
+        def stage0(unit):
+            launch(to_sibling(unit))
+
+        def stage1(unit):
+            for half in range(2):
+                landed(sib(unit, half), r_sib.at[unit, half])
+                ref, part_ref = sib(unit, half), part(unit, half, mine)
+
+                def put(spot, value, ref=ref):
+                    ref[spot, :] = value
+
+                add_into(put, lambda spot, ref=ref: ref[spot, :],
+                         lambda spot, part_ref=part_ref: part_ref[spot, :], deep)
+            launch(to_row(unit))
+
+        def stage2(unit):
+            landed(row_ref.at[unit], r_row.at[unit])
+            ref = sib(unit, row)
+
+            def put(spot, value):
+                row_ref[unit, spot, :] = value
+
+            add_into(put, lambda spot: row_ref[unit, spot, :], lambda spot: ref[spot, :], deep)
+            launch(to_x(unit))
+
+        def stage3(unit):
+            landed(x_ref.at[unit], r_x.at[unit])
+            ref = row_ref.at[unit, pl.ds(pl.multiple_of(xbit * half_deep, 16), half_deep)]
+
+            def put(spot, value):
+                x_ref[unit, spot, :] = value
+
+            add_into(put, lambda spot: x_ref[unit, spot, :], lambda spot: ref[spot, :], half_deep)
+            launch(to_z(unit))
+
+        def stage4(unit):
+            rows = pl.ds(pl.multiple_of(plane * small, 16), small)
+            total = x_ref[unit, rows, :].astype(jnp.float32)
+            for step in range(1, planes):
+                landed(z_ref.at[unit, step - 1], r_z.at[unit, step - 1])
+                total += z_ref[unit, step - 1].astype(jnp.float32)
+            spots = pl.ds(pl.multiple_of(xbit * half_deep + plane * small, 16), small)
+            res_ref[unit, spots, mine] = total.astype(jnp.bfloat16)
+            launch(along_z(unit))
+
+        def stage5(unit):
+            for step in range(1, planes):
+                landed(slab(unit, lax.rem(plane + planes - step, planes)), r_az.at[unit, step - 1])
+            launch(along_x(unit))
+
+        def stage6(unit):
+            rows = pl.ds(pl.multiple_of((1 - xbit) * half_deep, 16), half_deep)
+            landed(res_ref.at[unit, rows, mine], r_ax.at[unit])
+            launch(along_s(unit))
+            write_out(unit, 0, mine)
+
+        def stage7(unit):
+            landed(res_ref.at[unit, :, theirs], r_as.at[unit])
+            write_out(unit, 1, theirs)
+            for make in (to_sibling, to_row, to_x, to_z, along_z, along_x, along_s):
+                for copy in make(unit):
+                    copy.wait_send()
+
+        return stage0, stage1, stage2, stage3, stage4, stage5, stage6, stage7
+
+    early = pipeline(part_of, sib_of)
+    late = pipeline(qkv_part, qkv_sib)
+
+    def tick(stages, first, count, time):
+        for depth in range(1, 8):
+            unit = time - (depth - 1)
+
+            @pl.when((unit >= 0) & (unit < count))
+            def _(depth=depth, unit=unit):
+                stages[depth](first + unit)
+
+    def middle_part(act_ref, slope_ref, hid2, hid2_t, low_ref):
+        acc_ref = ingrad_ref
+        own_copy(1).wait()
+        chunk_done(2)
+        att_t = att_ref[...].reshape(width, BLOCK)
+        ap_ref[...] = product(transposed(att_t), wo[...])
+        gate_attn = mod_ref[:1, width : 2 * width]
+        scale_mlp = mod_ref[:1, 2 * width : 3 * width]
+        gate_mlp = mod_ref[:1, 3 * width :]
+        mid_ref[...] = tok_ref[...].astype(jnp.float32) + gate_attn * ap_ref[...]
+        normed, unused = layer_norm(mid_ref[...])
+        low = (normed * (1.0 + scale_mlp)).astype(jnp.bfloat16)
+        hid2[...] = low
+        hid2_t[...] = transposed(low)
+        acc_ref[...] = jnp.zeros_like(acc_ref)
+        own_copy(2).wait()
+        chunk_done(3)
+        for late_event in AFTER_EVENTS:
+            (pass_on, pass_last)[late_event[0]](late_event[1])
+        own_copy(3).wait()
+        chunk_done(4)
+        curve = math.sqrt(2.0 / math.pi)
+
+        def up(index, carry):
+            cols = pl.ds(pl.multiple_of(index * width, width), width)
+            before = product(hid2[...], wu[:, cols])
+            square = before * before
+            bent = jnp.tanh(curve * (before + 0.044715 * (square * before)))
+            after = (0.5 * before * (1.0 + bent)).astype(jnp.bfloat16)
+            act_ref[:, cols] = after
+            slope_ref[:, cols] = 0.5 * (1.0 + bent) + 0.5 * before * (1.0 - bent * bent) * (
+                curve * (1.0 + 3.0 * 0.044715 * square)
+            )
+            acc_ref[...] += product(after, wd[cols, :])
+            return carry
+
+        lax.fori_loop(0, 4, up, 0)
+        grad = cot_ref[...].astype(jnp.float32)
+        mlp_out = acc_ref[...]
+        result_ref[...] = mid_ref[...] + gate_mlp * mlp_out
+        sums_ref[3:4, :] = jnp.sum(grad * mlp_out, axis=0, keepdims=True)
+        low_ref[...] = (grad * gate_mlp).astype(jnp.bfloat16)
+        acc_ref[...] = jnp.zeros_like(acc_ref)
+
+        def down(index, carry):
+            for side in range(2):
+                cols = pl.ds(pl.multiple_of(side * 2 * width + index * width, width), width)
+                grad_act = product_back(low_ref[...], wd[cols, :])
+                grad_pre = (grad_act * slope_ref[:, cols]).astype(jnp.bfloat16)
+                grad_down = product(transposed(act_ref[:, cols]), low_ref[...])
+                for pick in range(2):
+                    parts[4 * index + pick, side] = grad_down[
+                        pick * deep : (pick + 1) * deep
+                    ].astype(jnp.bfloat16)
+                grad_up = product(hid2_t[...], grad_pre).astype(jnp.bfloat16)
+                for pick in range(2):
+                    for half in range(2):
+                        parts[4 * index + 2 + pick, half, :, side * span : (side + 1) * span] = (
+                            grad_up[half * deep : (half + 1) * deep, pick * span : (pick + 1) * span]
+                        )
+                acc_ref[...] += product_back(grad_pre, wu[:, cols])
+            for pick in range(4):
+                early[0](4 * index + pick)
+            return carry
+
+        lax.fori_loop(0, 2, down, 0)
+        for index in range(5):
+            if index > 1:
+                y_copy(index).wait_send()
+            onward(index, piece, 1, chip_next).wait_send()
+            onward(index, piece, 2, sibling).wait_send()
+            onward(index, jnp.bitwise_xor(piece, 2), 3, sibling).wait_send()
+        pl.semaphore_signal(free_sem, inc=1, device_id={"ctx": sibling}, device_id_type=MESH)
+        grad_hidden = acc_ref[...]
+        normed, inverse = layer_norm(mid_ref[...])
+        sums_ref[2:3, :] = jnp.sum(grad_hidden * normed, axis=0, keepdims=True)
+        grad_mid = cot_ref[...].astype(jnp.float32) + norm_back(
+            grad_hidden * (1.0 + scale_mlp), normed, inverse
+        )
+        ingrad_ref[...] = grad_mid
+        sums_ref[1:2, :] = jnp.sum(grad_mid * ap_ref[...], axis=0, keepdims=True)
+        gap = (grad_mid * gate_attn).astype(jnp.bfloat16)
+        low_ref[...] = gap
+        douts_ref[...] = product_back(wo[...], gap).astype(jnp.bfloat16).reshape(
+            heads, HD, BLOCK
+        )
+
+        def send_dout(step, carry):
+            send_head(lax.rem(step + 3 * plane, heads), douts_ref, got_ref, bs, br)
+            return carry
+
+        lax.fori_loop(0, heads, send_dout, 0)
+        grad_out = product(att_ref[...].reshape(width, BLOCK), low_ref[...]).astype(jnp.bfloat16)
+        parts[8, 0] = grad_out[:deep]
+        parts[8, 1] = grad_out[deep:]
+        early[0](8)
+
+    pl.run_scoped(
+        middle_part,
+        pltpu.VMEM((BLOCK, 4 * width), jnp.bfloat16),
+        pltpu.VMEM((BLOCK, 4 * width), jnp.float32),
+        pltpu.VMEM((BLOCK, width), jnp.bfloat16),
+        pltpu.VMEM((width, BLOCK), jnp.bfloat16),
+        pltpu.VMEM((BLOCK, width), jnp.bfloat16),
+    )
+
+    def backward(pair_ref, total_ref, low_ref):
+        @pl.when(owner)
+        def _():
+            def prepare(block, carry):
+                rows = pl.ds(pl.multiple_of(block * BLOCK, BLOCK), BLOCK)
+                pair_ref[rows, :] = transposed(buf_ref[block, HD:, :])
+                total_ref[rows, :] = jnp.zeros((BLOCK, 2 * HD), jnp.float32)
+                return carry
+
+            lax.fori_loop(0, blocks, prepare, 0)
+
+        def attend_back(block):
+            landed(got_ref.at[block], br.at[block])
+            dout = got_ref[block]
+            query = buf_ref[block, :HD, :]
+            zero = jnp.zeros((HD, BLOCK), jnp.bfloat16)
+            delta = jnp.sum(dout.astype(jnp.float32) * mix_ref[block], axis=0, keepdims=True)
+            lse = lse_ref[block, :1, :]
+            query_down = jnp.concatenate([query, zero], axis=0)
+            dout_down = jnp.concatenate([zero, dout], axis=0)
+            dout_side = transposed(jnp.concatenate([dout, zero], axis=0))
+            query_side = transposed(jnp.concatenate([zero, query], axis=0))
+
+            def key_block(key, grad_query):
+                key_rows = pl.ds(pl.multiple_of(key * BLOCK, BLOCK), BLOCK)
+                pair = pair_ref[key_rows, :]
+                probs = jnp.exp(product(pair, query_down) - lse)
+                grad_scores = (probs * (product(pair, dout_down) - delta)).astype(jnp.bfloat16)
+                total_ref[key_rows, :] += product(
+                    probs.astype(jnp.bfloat16), dout_side
+                ) + product(grad_scores, query_side)
+                return grad_query + product(buf_ref[key, HD : 2 * HD, :], grad_scores)
+
+            grad_query = lax.fori_loop(
+                0, block + 1, key_block, jnp.zeros((HD, BLOCK), jnp.float32)
+            )
+            rows = pl.ds(pl.multiple_of(block * BLOCK, BLOCK), BLOCK)
+            low_ref[block, :HD, :] = (grad_query * score_scale).astype(jnp.bfloat16)
+            sums = jnp.transpose(total_ref[rows, :]).astype(jnp.bfloat16)
+            low_ref[block, HD : 2 * HD, :] = sums[HD:]
+            low_ref[block, 2 * HD :, :] = sums[:HD]
+            return_block(me, head, block, low_ref, gland_ref, bbs, bbr)
+
+        def visit(step, carry):
+            @pl.when(owner)
+            def _():
+                attend_back(blocks - 1 - step)
+
+            tick(early, 0, 9, step - FIRST_TICK)
+            return carry
+
+        lax.fori_loop(0, blocks, visit, 0)
+
+        @pl.when(owner)
+        def _():
+            return_sent(me, head, blocks, low_ref, gland_ref, bbs, bbr)
+
+        scatter_sent(me, heads, douts_ref, got_ref, bs, br)
+        wait_heads(heads, gland_ref, bbr)
+
+    pl.run_scoped(
+        backward,
+        pltpu.VMEM((blocks * BLOCK, 2 * HD), jnp.bfloat16),
+        pltpu.VMEM((blocks * BLOCK, 2 * HD), jnp.float32),
+        pltpu.VMEM((blocks, 3 * HD, BLOCK), jnp.bfloat16),
+    )
+
+    def closing(gproj, acc_ref):
+        def turn_back(group, carry):
+            cos, sin = cos_ref[...], sin_ref[...]
+            for kind in range(3):
+                pieces = []
+                for inner in range(4):
+                    which = group * 4 + inner
+                    if kind == 2:
+                        pieces.append(gland_ref[which, 2 * HD :, :])
+                        continue
+                    top = gland_ref[which, kind * HD : kind * HD + HD // 2, :].astype(jnp.float32)
+                    bottom = gland_ref[
+                        which, kind * HD + HD // 2 : (kind + 1) * HD, :
+                    ].astype(jnp.float32)
+                    pieces.append((top * cos + bottom * sin).astype(jnp.bfloat16))
+                    pieces.append((bottom * cos - top * sin).astype(jnp.bfloat16))
+                cols = pl.ds(pl.multiple_of(kind * width + group * 4 * HD, 4 * HD), 4 * HD)
+                gproj[:, cols] = transposed(jnp.concatenate(pieces, axis=0))
+            return carry
+
+        lax.fori_loop(0, heads // 4, turn_back, 0)
+        acc_ref[...] = jnp.zeros_like(acc_ref)
+        pl.semaphore_wait(free_sem, 1)
+
+        def gradient(index, carry):
+            cols = pl.ds(pl.multiple_of(index * width, width), width)
+            low = product(hid1_t[...], gproj[:, cols]).astype(jnp.bfloat16)
+            wd[pl.ds(pl.multiple_of(index * width, width), width), :] = low
+            late[0](9 + index)
+            return carry
+
+        lax.fori_loop(0, 3, gradient, 0)
+
+        def back(index, carry):
+            cols = pl.ds(pl.multiple_of(index * width, width), width)
+            acc_ref[...] += product_back(gproj[:, cols], wq[:, cols])
+            return carry
+
+        tick(late, 9, 3, 0)
+        lax.fori_loop(0, 3, back, 0)
+        normed, inverse = layer_norm(tok_ref[...].astype(jnp.float32))
+        grad_hidden = acc_ref[...]
+        sums_ref[0:1, :] = jnp.sum(grad_hidden * normed, axis=0, keepdims=True)
+        ingrad_ref[...] = ingrad_ref[...] + norm_back(
+            grad_hidden * (1.0 + mod_ref[:1, :width]), normed, inverse
+        )
+
+    pl.run_scoped(
+        closing,
+        pltpu.VMEM((BLOCK, 3 * width), jnp.bfloat16),
+        pltpu.VMEM((BLOCK, width), jnp.float32),
+    )
+
+    def slots(first, count):
+        return table_ref.at[pl.ds(first, count)]
+
+    chip_slot = core * 4 * planes + 4 * plane
+
+    def table_row():
+        ref = slots(chip_slot + 2 * xbit + row, 1)
+        return [remote(ref, ref, s_t.at[0], r_t.at[0], fsdp=other)]
+
+    def table_x():
+        ref = slots(chip_slot + 2 * xbit, 2)
+        return [remote(ref, ref, s_t.at[1], r_t.at[1], ctx=chip_next)]
+
+    def table_z():
+        ref = slots(chip_slot, 4)
+        return [
+            remote(ref, ref, s_t.at[2 + step], r_t.at[2 + step],
+                   ctx=4 * lax.rem(plane + step, planes) + piece)
+            for step in range(1, planes)
+        ]
+
+    def table_s():
+        ref = slots(core * 4 * planes, 4 * planes)
+        return [remote(ref, ref, s_t.at[2], r_t.at[2], ctx=sibling)]
+
+    spot = chip_slot + 2 * xbit + row
+    for index in range(4):
+        table_ref[spot, index : index + 1, :] = sums_ref[index : index + 1, :]
+    table_ref[spot, 4:5, :] = emb_ref[:1, :]
+    for copy in table_row():
+        copy.start()
+
+    def finish(time, carry):
+        tick(late, 9, 3, time)
+
+        @pl.when(time == 1)
+        def _():
+            landed(slots(chip_slot + 2 * xbit + other, 1), r_t.at[0])
+            for copy in table_x():
+                copy.start()
+
+        @pl.when(time == 2)
+        def _():
+            landed(slots(chip_slot + 2 * (1 - xbit), 2), r_t.at[1])
+            for copy in table_z():
+                copy.start()
+
+        @pl.when(time == 4)
+        def _():
+            for step in range(1, planes):
+                goal = lax.rem(plane + planes - step, planes)
+                landed(slots(core * 4 * planes + 4 * goal, 4), r_t.at[2 + step])
+            for copy in table_s():
+                copy.start()
+
+        return carry
+
+    def rest(time, carry):
+        tick(early, 0, 9, time)
+        return carry
+
+    lax.fori_loop(blocks - FIRST_TICK, 15, rest, 0)
+    lax.fori_loop(1, 9, finish, 0)
+    landed(slots((1 - core) * 4 * planes, 4 * planes), r_t.at[2])
+    for copies in (table_row(), table_x(), table_z(), table_s()):
+        for copy in copies:
+            copy.wait_send()
+    for which in range(2):
+        pltpu.make_async_copy(
+            stage_ref.at[which], og_out.at[:, pl.ds(0, span)], out_sem.at[which]
+        ).wait()
+
+
+FORWARD_EVENTS = (
+    (1, (0, 2)),
+    (4, (1, 2)),
+    (8, (0, 3)),
+    (11, (1, 3)),
+    (13, (0, 4)),
+)
+AFTER_EVENTS = ((1, 4),)
+FIRST_TICK = 1
+
+
+def rope_constants(blocks):
+    half = HD // 2
+    frequency = rope_base ** (-2.0 * np.arange(half, dtype=np.float64) / HD)
+    inner = frequency[:, None] * np.arange(BLOCK, dtype=np.float64)[None, :]
+    outer = frequency[:, None] * (BLOCK * np.arange(128, dtype=np.float64))[None, :]
+    outer = np.where(np.arange(128)[None, :] < blocks, outer, 0.0)
+    return np.concatenate(
+        [np.cos(inner), np.sin(inner), np.cos(outer), np.sin(outer)], axis=1
+    ).astype(np.float32)
+
+
+def fast_device(tokens, timestep, time_table, w_qkv, w_out, w_up, w_down, w_ada, cotangent):
+    rows, width = tokens.shape[1:]
+    heads = width // HD
+    blocks = lax.axis_size("ctx")
+    planes = blocks // 4
+    deep, span = width // 2, width // 2
+    embedded = lax.dynamic_slice_in_dim(time_table, timestep[0, 0], 1, 0)
+    embedded = embedded.astype(jnp.bfloat16).astype(jnp.float32)
+    emb_rows = jnp.broadcast_to(embedded, (8, width))
+    hbm = pl.BlockSpec(memory_space=pl.ANY)
+    vmem = pl.BlockSpec(memory_space=pltpu.VMEM)
+    low, high = jnp.bfloat16, jnp.float32
+    dma = pltpu.SemaphoreType.DMA
+    steps = planes - 1
+    units = 12
+    scratch = [
+        pltpu.VMEM((width, 3 * width), low),
+        pltpu.VMEM((width, width), low),
+        pltpu.VMEM((width, 4 * width), low),
+        pltpu.VMEM((4 * width, width), low),
+        pltpu.VMEM((8, 4 * width), high),
+        pltpu.VMEM((8, width), high),
+        pltpu.VMEM((8, 4 * width), high),
+        pltpu.VMEM((8, 4 * width), high),
+        pltpu.VMEM((width, BLOCK), low),
+        pltpu.VMEM((BLOCK, width), high),
+        pltpu.VMEM((BLOCK, width), high),
+        pltpu.VMEM((8, width), high),
+        pltpu.VMEM((HD // 2, BLOCK), high),
+        pltpu.VMEM((HD // 2, BLOCK), high),
+        pltpu.VMEM((heads, 3 * HD, BLOCK), low),
+        pltpu.VMEM((blocks, 3 * HD, BLOCK), low),
+        pltpu.VMEM((blocks, HD, BLOCK), high),
+        pltpu.VMEM((blocks, 8, BLOCK), high),
+        pltpu.VMEM((heads, HD, BLOCK), low),
+        pltpu.VMEM((heads, HD, BLOCK), low),
+        pltpu.VMEM((blocks, HD, BLOCK), low),
+        pltpu.VMEM((9, 2, deep, width), low),
+        pltpu.VMEM((9, 2, deep, span), low),
+        pltpu.VMEM((units, deep, span), low),
+        pltpu.VMEM((units, deep // 2, span), low),
+        pltpu.VMEM((units, steps, deep // 2 // planes, span), low),
+        pltpu.VMEM((units, deep, width), low),
+        pltpu.VMEM((2, deep, span), high),
+    ]
+    sems = [
+        (5,), (2,), (2,), (5, 4), (5, 4),
+        (heads,), (blocks,), (blocks,), (heads,),
+        (heads,), (blocks,), (blocks,), (heads,),
+        (units, 2), (units, 2), (units,), (units,), (units,), (units,),
+        (units, steps), (units, steps), (units, steps), (units, steps),
+        (units,), (units,), (units,), (units,), (planes + 2,), (planes + 2,), (2,),
+    ]
+    scratch += [dma(shape) for shape in sems] + [pltpu.SemaphoreType.REGULAR]
+    result, input_grad, table, g_qkv, g_out, g_up, g_down = pl.pallas_call(
+        functools.partial(layer_kernel, blocks, heads),
+        out_shape=[
+            jax.ShapeDtypeStruct((rows, width), high),
+            jax.ShapeDtypeStruct((rows, width), high),
+            jax.ShapeDtypeStruct((2 * blocks, 8, width), high),
+        ]
+        + [jax.ShapeDtypeStruct(w.shape, high) for w in (w_qkv, w_out, w_up, w_down)],
+        in_specs=[vmem] * 4 + [hbm] * 5,
+        out_specs=[vmem] * 3 + [hbm] * 4,
+        scratch_shapes=scratch,
+        compiler_params=pltpu.CompilerParams(
+            collective_id=1, has_side_effects=True, vmem_limit_bytes=VMEM_LIMIT
+        ),
+    )(tokens[0], cotangent[0], emb_rows, jnp.asarray(rope_constants(blocks)),
+      w_ada, w_qkv, w_out, w_up, w_down)
+    shard_width = width // 2
+    embedded_part = lax.dynamic_slice_in_dim(
+        table[:, 4], lax.axis_index("fsdp") * shard_width, shard_width, 1
+    )
+    ada_total = lax.dot_general(
+        embedded_part, table[:, :4].reshape(2 * blocks, 4 * width), (((0,), (0,)), ((), ())),
+        precision=lax.Precision.HIGHEST,
+    )
+    return (result[None], input_grad[None], g_qkv, g_out, g_up, g_down, ada_total)
+
+
 def solution(mesh):
+    chosen = fast_device if mesh.shape["ctx"] == 16 else on_device
     return jax.shard_map(
-        on_device,
+        chosen,
         mesh=mesh,
         in_specs=(
             P("fsdp", "ctx", None),

time: 1390 us -> 343 us (0.25); the launches traced: 1370 us -> 340 us
  blocking collectives: 526 us -> 0 us
  Pallas kernels: 0 us -> 318 us
  waiting for transfers between devices: 255 us -> 0 us
  matrix products: 203 us -> 5.53 us
  local copies, waits for them, and re-layouts: 168 us -> 15 us
  loops' own time: 125 us -> 0 us
  other arithmetic: 74.6 us -> 0.76 us
  between operations: 15.7 us -> 1.36 us
    pallas_call x0 -> x1, Pallas kernels: none -> 318 us  [fast_device(): pl.pallas_call(functools.partial(layer_kernel, blocks, heads), out_shape=...]
    psum x1 -> x0, blocking collectives: 300 us -> none  [on_device(): totals = lax.psum((halves[0], halves[1], halves[2], halves[3]), 'ctx')]
    all_gather x9 -> x0, waiting for transfers between devices: 251 us -> none  [the longest x1 61.5 us: on_device(): lax.all_gather(key_own, 'ctx', axis=0, tiled=True)]
    all_gather x3 -> x0, blocking collectives: 226 us -> none  [the longest x1 90.9 us: on_device(): lax.all_gather(stat_rows, 'ctx', axis=0, tiled=True)]
    dot_general x68 -> x1, matrix products: 203 us -> 5.53 us  [fast_device(): lax.dot_general(embedded_part, table[:, :4].reshape(2 * blocks, 4 * width...]
    another operation x51 -> x0, loops' own time: 125 us -> none  [the longest x1 52.7 us: attend_forward(): lax.scan(attend_visit, partial_value, (split_rows(key_rows, sub_rows), sp...]
    dynamic_slice x49 -> x1, local copies, waits for them, and re-layouts: 62.8 us -> 0.03 us  [fast_device(): lax.dynamic_slice_in_dim(table[:, 4], lax.axis_index('fsdp') * shard_widt...]
    slice x49 -> x2, local copies, waits for them, and re-layouts: 57 us -> 2.55 us  [the longest x1 1.29 us: fast_device(): table[:, 4]]
  transfers between devices with their start and end apart: 13 -> 0, of which waited for: 5 -> 0; matrix products, arithmetic and copies ran while one was open for 32% -> 0% of each run, Pallas kernels for 0% -> 0%
where the time goes in v2:
time: 343 us; the launch traced here: 340 us
  Pallas kernels  318 us (93%)
  local copies, waits for them, and re-layouts  15 us (4%)
  matrix products  5.53 us (2%)
    pallas_call x1, Pallas kernels, fast_device(): pl.pallas_call(functools.partial(layer_kernel, blocks, heads), out_shape=...  318 us
    unnamed x23, local copies, waits for them, and re-layouts  11.8 us

profile of v2, /device:TPU:1, one launch (start us, length us, event | category | flops | bytes accessed | tf_op | source)
XLA Modules:
  0.0 340.4 jit_solution(10111755538888890315)
XLA Ops:
  1.3 0.8 convert_reduce_fusion
  2.0 0.6 broadcast_in_dim.18.emb_ref
  2.7 317.8 %shard_map.153 = (f32[256,768]{1,0:T(8,128)}, f32[256,768]{1,0:T(8,128)}, f32[32,8,768]{2,1,0:T(8,128)}, f32[384,2304]{1,0:T(8,128)}, f32[384,768]{1,0:T(8,128)}...) custom-call(bf16[256,768]{1,0:T(8,128)(2,1)} %bitcast.22, bf16[256,768]{1,0:T(8,128)(2,1)} %bitcast.23, ...), custom_call_target="tpu_custom_call" | custom-call | tf_op jit(solution)/shard_map/pallas_call | solution.py:1272
  320.4 0.0 copy-start.3
  320.4 1.3 slice.7
  321.7 0.1 copy.18
  321.8 0.0 copy-start.2
  321.8 1.3 slice.6
  323.1 0.0 copy-start
  323.1 5.5 %fusion = f32[384,3072]{1,0:T(8,128)} fusion(f32[32,3072]{1,0:T(8,128)S(1)} %bitcast.18, f32[32,1,384]{2,1,0:T(1,128)S(1)} %constant_dynamic-slice_fusion), kind=kOutput, calls=%fused_computation | convolution fusion | flops 452984832 | bytes 5160960 | tf_op jit(solution)/shard_map/dot_general | solution.py:1292
  328.6 0.0 copy-done.3
  328.6 0.9 copy.30
  329.5 0.0 copy-done.2
  329.5 0.9 copy.31
  330.4 0.0 copy-done
  330.4 1.8 copy.32
  332.2 1.4 copy-done.1
  333.6 1.0 copy.33
  334.6 0.0 slice-done.2
  334.6 0.0 slice-done.3
  334.7 2.4 copy.34
  337.1 0.8 slice-done
  337.9 0.3 slice-done.1
  338.2 2.2 copy.35
  (8 shorter events, 0.0 us)
Async XLA Ops:
  320.4 8.2 %copy-start.3 = (f32[256,768]{1,0:T(8,128)S(1)}, f32[256,768]{1,0:T(8,128)}, u32[]{:S(2)}) copy-start(f32[256,768]{1,0:T(8,128)} %get-tuple-element.14) | copy-start | bytes 2359300
  321.8 7.8 %copy-start.2 = (f32[256,768]{1,0:T(8,128)S(1)}, f32[256,768]{1,0:T(8,128)}, u32[]{:S(2)}) copy-start(f32[256,768]{1,0:T(8,128)} %get-tuple-element.15) | copy-start | bytes 2359300
  323.1 7.3 %copy-start = (f32[384,2304]{1,0:T(8,128)S(1)}, f32[384,2304]{1,0:T(8,128)}, u32[]{:S(2)}) copy-start(f32[384,2304]{1,0:T(8,128)} %get-tuple-element.30) | copy-start | bytes 10616836
  329.5 5.1 %slice-start.2 = ((s8[4718592]{0:T(1024)(128)(4,1)}), s8[4194304]{0:T(1024)(128)(4,1)S(1)}, s32[]{:S(2)}) async-start(s8[4718592]{0:T(1024)(128)(4,1)} %bitcast.16), calls=%async_computation.2 | async-start | bytes 8388608
  330.4 3.2 copy-start.1
  330.4 4.2 %slice-start.3 = ((s8[4718592]{0:T(1024)(128)(4,1)}), s8[524288]{0:T(1024)(128)(4,1)S(1)}, s32[]{:S(2)}) async-start(s8[4718592]{0:T(1024)(128)(4,1)} %bitcast.16), calls=%async_computation.3 | async-start | bytes 1048576
  333.6 4.3 %slice-start = ((s8[4718592]{0:T(1024)(128)(4,1)}), s8[4194304]{0:T(1024)(128)(4,1)S(1)}, s32[]{:S(2)}) async-start(s8[4718592]{0:T(1024)(128)(4,1)} %bitcast.14), calls=%async_computation | async-start | bytes 8388608
  334.6 3.5 %slice-start.1 = ((s8[4718592]{0:T(1024)(128)(4,1)}), s8[524288]{0:T(1024)(128)(4,1)S(1)}, s32[]{:S(2)}) async-start(s8[4718592]{0:T(1024)(128)(4,1)} %bitcast.14), calls=%async_computation.1 | async-start | bytes 1048576

commit v3 on v2

--- a/solution.py
+++ b/solution.py
@@ -460,11 +460,11 @@
 def layer_kernel(
     blocks, heads,
     tok_ref, cot_ref, emb_ref, rope_ref, ada_hbm, qkv_hbm, out_hbm, up_hbm, down_hbm,
-    result_ref, ingrad_ref, table_ref, og_qkv, og_out, og_up, og_down,
+    result_ref, ingrad_ref, eds_ref, sds_ref, og_qkv, og_out, og_up, og_down,
     wq, wo, wu, wd, mod_ref, emb_other, part_other, part_send,
     hid1_t, mid_ref, ap_ref, sums_ref, cos_ref, sin_ref,
     qs_ref, buf_ref, mix_ref, lse_ref, att_ref, douts_ref, got_ref,
-    parts, sib_ref, row_ref, x_ref, z_ref, res_ref, stage_ref,
+    parts, sib_ref, row_ref, x_ref, z_ref, res_ref, table_ref,
     own_sem, small_send, small_recv, w_send, w_recv,
     fs, fr, fbs, fbr, bs, br, bbs, bbr,
     s_sib, r_sib, s_row, r_row, s_x, r_x, s_z, r_z, s_az, r_az, s_ax, r_ax, s_as, r_as,
@@ -500,26 +500,31 @@
     shards = (qkv_hbm, out_hbm, up_hbm, down_hbm)
     wholes = (wq, wo, wu, wd)
     quarter_rows = [shard.shape[0] // 4 for shard in shards]
+    third = quarter_rows[0] // 3
     chunks = [
-        (0, 0, quarter_rows[0] // 2),
-        (0, quarter_rows[0] // 2, quarter_rows[0] // 2),
+        (0, 0, third),
+        (0, third, third),
+        (0, 2 * third, third),
         (1, 0, quarter_rows[1]),
         (2, 0, quarter_rows[2]),
-        (3, 0, quarter_rows[3]),
+        (3, 0, 2 * quarter_rows[3]),
     ]
+
+    def chunk_start(index, half, which):
+        weight, first, count = chunks[index]
+        if index == 5:
+            return pl.multiple_of(half * 2 * count + lax.rem(which, 2) * count, 16)
+        return pl.multiple_of((half * 4 + which) * quarter_rows[weight] + first, 16)
 
     def chunk_ref(index, which):
         weight, first, count = chunks[index]
-        start = other * 4 * quarter_rows[weight] + which * quarter_rows[weight] + first
-        return wholes[weight].at[pl.ds(pl.multiple_of(start, 16), count)]
+        return wholes[weight].at[pl.ds(chunk_start(index, other, which), count)]
 
     def y_copy(index):
         weight, first, count = chunks[index]
-        near = piece * quarter_rows[weight] + first
-        far = row * 4 * quarter_rows[weight] + near
         return remote(
-            shards[weight].at[pl.ds(pl.multiple_of(near, 16), count)],
-            wholes[weight].at[pl.ds(pl.multiple_of(far, 16), count)],
+            shards[weight].at[pl.ds(chunk_start(index, 0, piece), count)],
+            wholes[weight].at[pl.ds(chunk_start(index, row, piece), count)],
             w_send.at[index, 0], w_recv.at[index, 0], fsdp=other,
         )
 
@@ -529,7 +534,8 @@
 
     def pass_on(index):
         landed(chunk_ref(index, piece), w_recv.at[index, 0])
-        onward(index, piece, 1, chip_next).start()
+        if index < 5:
+            onward(index, piece, 1, chip_next).start()
         onward(index, piece, 2, sibling).start()
 
     def pass_last(index):
@@ -539,7 +545,15 @@
 
     def chunk_done(index):
         landed(chunk_ref(index, jnp.bitwise_xor(piece, 1)), w_recv.at[index, 2])
-        landed(chunk_ref(index, jnp.bitwise_xor(piece, 3)), w_recv.at[index, 3])
+        if index < 5:
+            landed(chunk_ref(index, jnp.bitwise_xor(piece, 3)), w_recv.at[index, 3])
+
+    def chunk_sent(index):
+        y_copy(index).wait_send()
+        onward(index, piece, 2, sibling).wait_send()
+        if index < 5:
+            onward(index, piece, 1, chip_next).wait_send()
+            onward(index, jnp.bitwise_xor(piece, 2), 3, sibling).wait_send()
 
     def own_copy(weight):
         half = shards[weight].shape[0]
@@ -550,14 +564,16 @@
 
     emb_copy = remote(emb_ref, emb_other, small_send.at[0], small_recv.at[0], fsdp=other)
     emb_copy.start()
-    y_copy(0).start()
-    y_copy(1).start()
+    for index in range(5):
+        y_copy(index).start()
 
     def opening(ada_ref, hid1):
         ada_copy = pltpu.make_async_copy(ada_hbm, ada_ref, own_sem.at[4])
         ada_copy.start()
         for weight in range(4):
             own_copy(weight).start()
+        normed, unused = layer_norm(tok_ref[...].astype(jnp.float32))
+        ingrad_ref[...] = normed
         half_width = width // 2
         cols = pl.ds(pl.multiple_of(row * half_width, 128), half_width)
         ada_copy.wait()
@@ -568,31 +584,31 @@
         part_send[...] = partial[8:]
         part_copy = remote(part_send, part_other, small_send.at[1], small_recv.at[1], fsdp=other)
         part_copy.start()
+        pass_on(0)
         lanes = lax.broadcasted_iota(jnp.int32, (HD // 2, 128), 1)
         pick = lanes == me
-        cos_block = jnp.sum(jnp.where(pick, rope_ref[:, 2 * BLOCK : 2 * BLOCK + 128], 0.0), axis=1, keepdims=True)
-        sin_block = jnp.sum(jnp.where(pick, rope_ref[:, 2 * BLOCK + 128 :], 0.0), axis=1, keepdims=True)
+        cos_block = jnp.sum(
+            jnp.where(pick, rope_ref[:, 2 * BLOCK : 2 * BLOCK + 128], 0.0), axis=1, keepdims=True
+        )
+        sin_block = jnp.sum(
+            jnp.where(pick, rope_ref[:, 2 * BLOCK + 128 :], 0.0), axis=1, keepdims=True
+        )
         cos_row = rope_ref[:, :BLOCK]
         sin_row = rope_ref[:, BLOCK : 2 * BLOCK]
         cos_ref[...] = cos_row * cos_block - sin_row * sin_block
         sin_ref[...] = sin_row * cos_block + cos_row * sin_block
-        pass_on(0)
-        normed, unused = layer_norm(tok_ref[...].astype(jnp.float32))
         part_copy.wait()
         mod_ref[...] += part_other[...]
-        low = (normed * (1.0 + mod_ref[:1, :width])).astype(jnp.bfloat16)
+        low = (ingrad_ref[...] * (1.0 + mod_ref[:1, :width])).astype(jnp.bfloat16)
         hid1[...] = low
+        pass_on(1)
         hid1_t[...] = transposed(low)
-        pass_on(1)
-        pass_last(0)
-        pass_last(1)
-        for index in (0, 1):
-            y_copy(index).wait_send()
-        for index in (2, 3, 4):
-            y_copy(index).start()
+        pass_on(2)
+        for index in range(3):
+            pass_last(index)
         own_copy(0).wait()
-        chunk_done(0)
-        chunk_done(1)
+        for index in range(3):
+            chunk_done(index)
 
         def project(group, carry):
             spans = []
@@ -614,10 +630,17 @@
                 qs_ref[which, 2 * HD :, :] = spans[2][inner * HD : (inner + 1) * HD].astype(
                     jnp.bfloat16
                 )
-                send_head(which, qs_ref, buf_ref, fs, fr)
             return carry
 
         lax.fori_loop(0, heads // 4, project, 0)
+
+        def send_block(step, carry):
+            send_head(lax.rem(step + 3 * (plane + 2), heads), qs_ref, buf_ref, fs, fr)
+            return carry
+
+        lax.fori_loop(0, heads, send_block, 0)
+        y_copy(5).start()
+        pass_on(3)
 
     def send_head(which, source, target, send_sem, recv_sem):
         goal = head_owner(which)
@@ -639,56 +662,71 @@
     )
 
     def forward(pair_ref, low_ref):
-        def attend(block):
-            landed(buf_ref.at[block], fr.at[block])
-            rows = pl.ds(pl.multiple_of(block * BLOCK, BLOCK), BLOCK)
-            pair_ref[rows, :] = transposed(buf_ref[block, HD:, :])
-            query = jnp.concatenate(
-                [buf_ref[block, :HD, :], jnp.zeros((HD, BLOCK), jnp.bfloat16)], axis=0
-            )
-
-            def key_block(key, state):
-                high, total, mixed = state
-                key_rows = pl.ds(pl.multiple_of(key * BLOCK, BLOCK), BLOCK)
-                scores = product(pair_ref[key_rows, :], query)
-                new_high = jnp.maximum(high, jnp.max(scores, axis=0, keepdims=True))
-                weights = jnp.exp(scores - new_high)
-                decay = jnp.exp(high - new_high)
-                total = total * decay + jnp.sum(weights, axis=0, keepdims=True)
-                mixed = mixed * decay + product(
-                    buf_ref[key, 2 * HD :, :], weights.astype(jnp.bfloat16)
+        def value_of(key):
+            ones = jnp.ones((16, BLOCK), jnp.bfloat16)
+            return jnp.concatenate([buf_ref[key, 2 * HD :, :], ones], axis=0)
+
+        def attend(group):
+            first = 4 * group
+            for inner in range(4):
+                block = first + inner
+                landed(buf_ref.at[block], fr.at[block])
+                rows = pl.ds(pl.multiple_of(block * BLOCK, BLOCK), BLOCK)
+                pair_ref[rows, :] = transposed(buf_ref[block, HD:, :])
+            query = side_by_side(lambda block: buf_ref[block, :HD, :], first)
+            query = jnp.concatenate([query, jnp.zeros_like(query)], axis=0)
+
+            def step(state, key, count, skip):
+                high, mixed = state
+                rows = pl.ds(pl.multiple_of(key * BLOCK, BLOCK), count * BLOCK)
+                begin = (skip or 0) * BLOCK
+                scores = product(pair_ref[rows, :], query[:, begin:])
+                if skip is not None:
+                    scores = jnp.where(seen(scores.shape), scores, masked_score)
+                new_high = jnp.maximum(high[:, begin:], jnp.max(scores, axis=0, keepdims=True))
+                weights = jnp.exp(scores - new_high).astype(jnp.bfloat16)
+                values = jnp.concatenate([value_of(key + index) for index in range(count)], axis=1)
+                new_mixed = mixed[:, begin:] * jnp.exp(high[:, begin:] - new_high) + product(
+                    values, weights
                 )
-                return new_high, total, mixed
-
-            high, total, mixed = lax.fori_loop(
-                0,
-                block + 1,
-                key_block,
-                (
-                    jnp.full((1, BLOCK), masked_score, jnp.float32),
-                    jnp.zeros((1, BLOCK), jnp.float32),
-                    jnp.zeros((HD, BLOCK), jnp.float32),
-                ),
-            )
-            mixed = mixed / total
-            mix_ref[block] = mixed
-            low_ref[block] = mixed.astype(jnp.bfloat16)
-            lse_ref[block] = jnp.broadcast_to(high + jnp.log(total), (8, BLOCK))
-            return_block(me, head, block, low_ref, att_ref, fbs, fbr)
-
-        def visit(block, carry):
+                if begin:
+                    new_high = jnp.concatenate([high[:, :begin], new_high], axis=1)
+                    new_mixed = jnp.concatenate([mixed[:, :begin], new_mixed], axis=1)
+                return new_high, new_mixed
+
+            state = (
+                jnp.full((1, 4 * BLOCK), masked_score, jnp.float32),
+                jnp.zeros((HD + 16, 4 * BLOCK), jnp.float32),
+            )
+            state = lax.fori_loop(
+                0, group, lambda index, now: step(now, 4 * index, 4, None), state
+            )
+            state = step(state, first, 2, 0)
+            high, mixed = step(state, first + 2, 2, 2)
+            total = mixed[HD : HD + 1]
+            mixed = mixed[:HD] / total
+            lse = high + jnp.log(total)
+            for inner in range(4):
+                block = first + inner
+                cols = slice(inner * BLOCK, (inner + 1) * BLOCK)
+                mix_ref[block] = mixed[:, cols]
+                low_ref[block] = mixed[:, cols].astype(jnp.bfloat16)
+                lse_ref[block] = jnp.broadcast_to(lse[:, cols], (8, BLOCK))
+                return_block(me, head, block, low_ref, att_ref, fbs, fbr)
+
+        def visit(group, carry):
             @pl.when(owner)
             def _():
-                attend(block)
+                attend(group)
 
             for when, event in FORWARD_EVENTS:
-                @pl.when(block == when)
+                @pl.when(group == when)
                 def _(event=event):
                     (pass_on, pass_last)[event[0]](event[1])
 
             return carry
 
-        lax.fori_loop(0, blocks, visit, 0)
+        lax.fori_loop(0, blocks // 4, visit, 0)
 
         @pl.when(owner)
         def _():
@@ -777,31 +815,18 @@
                 copy.start()
 
         def write_out(unit, which, cols):
-            def saved():
-                return pltpu.make_async_copy(
-                    stage_ref.at[which], og_out.at[:, pl.ds(0, span)], out_sem.at[which]
-                )
-
-            @pl.when(unit > 0)
-            def _():
-                saved().wait()
-
-            def convert(index, carry):
-                spot = pl.ds(pl.multiple_of(index * 48, 48), 48)
-                stage_ref[which, spot, :] = res_ref[unit, spot, cols].astype(jnp.float32)
-                return carry
-
-            lax.fori_loop(0, deep // 48, convert, 0)
             side = core if which == 0 else 1 - core
             kind = lax.rem(unit, 4)
             order = 2 * (unit // 4) + lax.rem(kind, 2)
 
             def save(target):
-                pltpu.make_async_copy(stage_ref.at[which], target, out_sem.at[which]).start()
+                pltpu.make_async_copy(
+                    res_ref.at[unit, :, cols], target, out_sem.at[unit, which]
+                ).start()
 
             @pl.when((unit < 8) & (kind < 2))
             def _():
-                save(og_down.at[pl.ds(pl.multiple_of(order * deep, 8), deep),
+                save(og_down.at[pl.ds(pl.multiple_of(order * deep, 16), deep),
                                 pl.ds(pl.multiple_of(side * span, 128), span)])
 
             @pl.when((unit < 8) & (kind >= 2))
@@ -842,6 +867,9 @@
 
             add_into(put, lambda spot: row_ref[unit, spot, :], lambda spot: ref[spot, :], deep)
             launch(to_x(unit))
+            for make in (to_sibling, to_row):
+                for copy in make(unit):
+                    copy.wait_send()
 
         def stage3(unit):
             landed(x_ref.at[unit], r_x.at[unit])
@@ -877,7 +905,7 @@
         def stage7(unit):
             landed(res_ref.at[unit, :, theirs], r_as.at[unit])
             write_out(unit, 1, theirs)
-            for make in (to_sibling, to_row, to_x, to_z, along_z, along_x, along_s):
+            for make in (to_x, to_z, along_z, along_x, along_s):
                 for copy in make(unit):
                     copy.wait_send()
 
@@ -886,18 +914,34 @@
     early = pipeline(part_of, sib_of)
     late = pipeline(qkv_part, qkv_sib)
 
-    def tick(stages, first, count, time):
-        for depth in range(1, 8):
-            unit = time - (depth - 1)
-
-            @pl.when((unit >= 0) & (unit < count))
-            def _(depth=depth, unit=unit):
-                stages[depth](first + unit)
+    def tick(time, carry):
+        for stage, lag in ((1, 0), (2, 2)):
+            unit = time - lag
+
+            @pl.when((unit >= 0) & (unit < 9))
+            def _(stage=stage, unit=unit):
+                early[stage](unit)
+
+            @pl.when((unit >= 9) & (unit < 12))
+            def _(stage=stage, unit=unit):
+                late[stage](unit)
+
+        for stage in range(3, 8):
+            unit = time - stage
+
+            @pl.when((unit >= 0) & (unit < 12))
+            def _(stage=stage, unit=unit):
+                early[stage](unit)
+
+        return carry
+
+    def ticks(first, last):
+        lax.fori_loop(first, last, tick, 0)
 
     def middle_part(act_ref, slope_ref, hid2, hid2_t, low_ref):
         acc_ref = ingrad_ref
         own_copy(1).wait()
-        chunk_done(2)
+        chunk_done(3)
         att_t = att_ref[...].reshape(width, BLOCK)
         ap_ref[...] = product(transposed(att_t), wo[...])
         gate_attn = mod_ref[:1, width : 2 * width]
@@ -910,11 +954,9 @@
         hid2_t[...] = transposed(low)
         acc_ref[...] = jnp.zeros_like(acc_ref)
         own_copy(2).wait()
-        chunk_done(3)
-        for late_event in AFTER_EVENTS:
-            (pass_on, pass_last)[late_event[0]](late_event[1])
+        chunk_done(4)
         own_copy(3).wait()
-        chunk_done(4)
+        chunk_done(5)
         curve = math.sqrt(2.0 / math.pi)
 
         def up(index, carry):
@@ -960,12 +1002,8 @@
             return carry
 
         lax.fori_loop(0, 2, down, 0)
-        for index in range(5):
-            if index > 1:
-                y_copy(index).wait_send()
-            onward(index, piece, 1, chip_next).wait_send()
-            onward(index, piece, 2, sibling).wait_send()
-            onward(index, jnp.bitwise_xor(piece, 2), 3, sibling).wait_send()
+        for index in range(len(chunks)):
+            chunk_sent(index)
         pl.semaphore_signal(free_sem, inc=1, device_id={"ctx": sibling}, device_id_type=MESH)
         grad_hidden = acc_ref[...]
         normed, inverse = layer_norm(mid_ref[...])
@@ -982,10 +1020,12 @@
         )
 
         def send_dout(step, carry):
-            send_head(lax.rem(step + 3 * plane, heads), douts_ref, got_ref, bs, br)
+            send_head(lax.rem(step + 3 * (plane + 2), heads), douts_ref, got_ref, bs, br)
             return carry
 
+        early[1](0)
         lax.fori_loop(0, heads, send_dout, 0)
+        early[1](1)
         grad_out = product(att_ref[...].reshape(width, BLOCK), low_ref[...]).astype(jnp.bfloat16)
         parts[8, 0] = grad_out[:deep]
         parts[8, 1] = grad_out[deep:]
@@ -1000,70 +1040,134 @@
         pltpu.VMEM((BLOCK, width), jnp.bfloat16),
     )
 
-    def backward(pair_ref, total_ref, low_ref):
+    def backward(both_ref, side_ref, grad_ref, lse_wide, delta_wide, low_ref):
         @pl.when(owner)
         def _():
-            def prepare(block, carry):
-                rows = pl.ds(pl.multiple_of(block * BLOCK, BLOCK), BLOCK)
-                pair_ref[rows, :] = transposed(buf_ref[block, HD:, :])
-                total_ref[rows, :] = jnp.zeros((BLOCK, 2 * HD), jnp.float32)
+            def prepare(group, carry):
+                first = 4 * group
+                for inner in range(4):
+                    landed(got_ref.at[first + inner], br.at[first + inner])
+                dout = side_by_side(lambda block: got_ref[block], first)
+                query = side_by_side(lambda block: buf_ref[block, :HD, :], first)
+                mixed = side_by_side(lambda block: mix_ref[block], first)
+                both = jnp.concatenate([query, dout], axis=0)
+                both_ref[group] = both
+                side_ref[group] = transposed(both)
+                grad_ref[group] = jnp.zeros((HD, 4 * BLOCK), jnp.float32)
+                lse_wide[group] = side_by_side(lambda block: lse_ref[block], first)
+                delta = jnp.sum(dout.astype(jnp.float32) * mixed, axis=0, keepdims=True)
+                delta_wide[group] = jnp.broadcast_to(delta, (8, 4 * BLOCK))
                 return carry
 
-            lax.fori_loop(0, blocks, prepare, 0)
-
-        def attend_back(block):
-            landed(got_ref.at[block], br.at[block])
-            dout = got_ref[block]
-            query = buf_ref[block, :HD, :]
-            zero = jnp.zeros((HD, BLOCK), jnp.bfloat16)
-            delta = jnp.sum(dout.astype(jnp.float32) * mix_ref[block], axis=0, keepdims=True)
-            lse = lse_ref[block, :1, :]
-            query_down = jnp.concatenate([query, zero], axis=0)
-            dout_down = jnp.concatenate([zero, dout], axis=0)
-            dout_side = transposed(jnp.concatenate([dout, zero], axis=0))
-            query_side = transposed(jnp.concatenate([zero, query], axis=0))
-
-            def key_block(key, grad_query):
-                key_rows = pl.ds(pl.multiple_of(key * BLOCK, BLOCK), BLOCK)
-                pair = pair_ref[key_rows, :]
-                probs = jnp.exp(product(pair, query_down) - lse)
-                grad_scores = (probs * (product(pair, dout_down) - delta)).astype(jnp.bfloat16)
-                total_ref[key_rows, :] += product(
-                    probs.astype(jnp.bfloat16), dout_side
-                ) + product(grad_scores, query_side)
-                return grad_query + product(buf_ref[key, HD : 2 * HD, :], grad_scores)
-
-            grad_query = lax.fori_loop(
-                0, block + 1, key_block, jnp.zeros((HD, BLOCK), jnp.float32)
-            )
-            rows = pl.ds(pl.multiple_of(block * BLOCK, BLOCK), BLOCK)
-            low_ref[block, :HD, :] = (grad_query * score_scale).astype(jnp.bfloat16)
-            sums = jnp.transpose(total_ref[rows, :]).astype(jnp.bfloat16)
-            low_ref[block, HD : 2 * HD, :] = sums[HD:]
-            low_ref[block, 2 * HD :, :] = sums[:HD]
-            return_block(me, head, block, low_ref, gland_ref, bbs, bbr)
-
-        def visit(step, carry):
-            @pl.when(owner)
+            lax.fori_loop(0, blocks // 4, prepare, 0)
+
+        def key_back(group, inner):
+            key = 4 * group + inner
+            pair = transposed(buf_ref[key, HD:, :])
+            left = lax.broadcasted_iota(jnp.int32, pair.shape, 1) < HD
+            none = jnp.zeros_like(pair)
+            key_side, value_side = jnp.where(left, pair, none), jnp.where(left, none, pair)
+            key_low = buf_ref[key, HD : 2 * HD, :]
+
+            def visit_queries(which, skip, state):
+                begin = skip * BLOCK
+                both = both_ref[which, :, begin:]
+                probs = jnp.exp(product(key_side, both) - lse_wide[which, :1, begin:])
+                grad_scores = (
+                    probs * (product(value_side, both) - delta_wide[which, :1, begin:])
+                ).astype(jnp.bfloat16)
+                side = side_ref[which, begin:, :]
+                grad_ref[which, :, begin:] += product(key_low, grad_scores)
+                return (
+                    state[0] + product(grad_scores, side),
+                    state[1] + product(probs.astype(jnp.bfloat16), side),
+                )
+
+            zero = jnp.zeros((BLOCK, 2 * HD), jnp.float32)
+            state = visit_queries(group, inner, (zero, zero))
+            state = lax.fori_loop(
+                group + 1, blocks // 4, lambda which, now: visit_queries(which, 0, now), state
+            )
+            low_ref[key, HD : 2 * HD, :] = jnp.transpose(state[0])[:HD].astype(jnp.bfloat16)
+            low_ref[key, 2 * HD :, :] = jnp.transpose(state[1])[HD:].astype(jnp.bfloat16)
+            return_rows(key, HD, 2 * HD, 0)
+
+        def part_copy_of(block, first, count, slot):
+            return remote(
+                low_ref.at[block, pl.ds(first, count)], gland_ref.at[head, pl.ds(first, count)],
+                bbs.at[block, slot], bbr.at[head, slot], ctx=block,
+            )
+
+        def return_rows(block, first, count, slot):
+            @pl.when(block != me)
             def _():
-                attend_back(blocks - 1 - step)
-
-            tick(early, 0, 9, step - FIRST_TICK)
-            return carry
-
-        lax.fori_loop(0, blocks, visit, 0)
+                part_copy_of(block, first, count, slot).start()
+
+            @pl.when(block == me)
+            def _():
+                pltpu.make_async_copy(
+                    low_ref.at[block, pl.ds(first, count)],
+                    gland_ref.at[head, pl.ds(first, count)],
+                    bbr.at[head, slot],
+                ).start()
+
+        begun = 2
+        for inner in range(4):
+            def visit(group, carry, inner=inner):
+                @pl.when(owner)
+                def _():
+                    key_back(group, inner)
+
+                return carry
+
+            for edge in range(len(TICKS[inner])):
+                low, high = SPLITS[edge], SPLITS[edge + 1]
+                lax.fori_loop(low, high, visit, 0)
+                ticks(begun, begun + TICKS[inner][edge])
+                begun += TICKS[inner][edge]
 
         @pl.when(owner)
         def _():
-            return_sent(me, head, blocks, low_ref, gland_ref, bbs, bbr)
+            def finish_query(group, carry):
+                grad_query = (grad_ref[group] * score_scale).astype(jnp.bfloat16)
+                for inner in range(4):
+                    block = 4 * group + inner
+                    low_ref[block, :HD, :] = grad_query[:, inner * BLOCK : (inner + 1) * BLOCK]
+                    return_rows(block, 0, HD, 1)
+                return carry
+
+            lax.fori_loop(0, blocks // 4, finish_query, 0)
+
+        ticks(begun, begun + TICKS[4][0])
+
+        @pl.when(owner)
+        def _():
+            def sent(block, carry):
+                @pl.when(block != me)
+                def _():
+                    part_copy_of(block, HD, 2 * HD, 0).wait_send()
+                    part_copy_of(block, 0, HD, 1).wait_send()
+
+                return carry
+
+            lax.fori_loop(0, blocks, sent, 0)
 
         scatter_sent(me, heads, douts_ref, got_ref, bs, br)
-        wait_heads(heads, gland_ref, bbr)
+
+        def arrived(which, carry):
+            landed(gland_ref.at[which, pl.ds(HD, 2 * HD)], bbr.at[which, 0])
+            landed(gland_ref.at[which, pl.ds(0, HD)], bbr.at[which, 1])
+            return carry
+
+        lax.fori_loop(0, heads, arrived, 0)
 
     pl.run_scoped(
         backward,
-        pltpu.VMEM((blocks * BLOCK, 2 * HD), jnp.bfloat16),
-        pltpu.VMEM((blocks * BLOCK, 2 * HD), jnp.float32),
+        pltpu.VMEM((blocks // 4, 2 * HD, 4 * BLOCK), jnp.bfloat16),
+        pltpu.VMEM((blocks // 4, 4 * BLOCK, 2 * HD), jnp.bfloat16),
+        pltpu.VMEM((blocks // 4, HD, 4 * BLOCK), jnp.float32),
+        pltpu.VMEM((blocks // 4, 8, 4 * BLOCK), jnp.float32),
+        pltpu.VMEM((blocks // 4, 8, 4 * BLOCK), jnp.float32),
         pltpu.VMEM((blocks, 3 * HD, BLOCK), jnp.bfloat16),
     )
 
@@ -1105,7 +1209,6 @@
             acc_ref[...] += product_back(gproj[:, cols], wq[:, cols])
             return carry
 
-        tick(late, 9, 3, 0)
         lax.fori_loop(0, 3, back, 0)
         normed, inverse = layer_norm(tok_ref[...].astype(jnp.float32))
         grad_hidden = acc_ref[...]
@@ -1152,22 +1255,24 @@
     for copy in table_row():
         copy.start()
 
+    begun = 2 + sum(sum(counts) for counts in TICKS)
+
     def finish(time, carry):
-        tick(late, 9, 3, time)
-
-        @pl.when(time == 1)
+        tick(time, carry)
+
+        @pl.when(time == begun + 1)
         def _():
             landed(slots(chip_slot + 2 * xbit + other, 1), r_t.at[0])
             for copy in table_x():
                 copy.start()
 
-        @pl.when(time == 2)
+        @pl.when(time == begun + 3)
         def _():
             landed(slots(chip_slot + 2 * (1 - xbit), 2), r_t.at[1])
             for copy in table_z():
                 copy.start()
 
-        @pl.when(time == 4)
+        @pl.when(time == begun + 5)
         def _():
             for step in range(1, planes):
                 goal = lax.rem(plane + planes - step, planes)
@@ -1177,31 +1282,53 @@
 
         return carry
 
-    def rest(time, carry):
-        tick(early, 0, 9, time)
-        return carry
-
-    lax.fori_loop(blocks - FIRST_TICK, 15, rest, 0)
-    lax.fori_loop(1, 9, finish, 0)
+    lax.fori_loop(begun, 19, finish, 0)
     landed(slots((1 - core) * 4 * planes, 4 * planes), r_t.at[2])
+    count = 2 * blocks
+    emb_cols = pl.ds(pl.multiple_of(row * (width // 2), 128), width // 2)
+    eds = table_ref[:, 4, emb_cols].astype(jnp.bfloat16)
+    for third_part in range(3):
+        eds_ref[third_part * count : (third_part + 1) * count, :] = eds
+    for index in range(4):
+        left = table_ref[:, index, :]
+        for third_part in range(3):
+            low = left.astype(jnp.bfloat16)
+            left = left - low.astype(jnp.float32)
+            sds_ref[
+                third_part * count : (third_part + 1) * count, index * width : (index + 1) * width
+            ] = low
     for copies in (table_row(), table_x(), table_z(), table_s()):
         for copy in copies:
             copy.wait_send()
-    for which in range(2):
-        pltpu.make_async_copy(
-            stage_ref.at[which], og_out.at[:, pl.ds(0, span)], out_sem.at[which]
-        ).wait()
+
+    def saved(unit, carry):
+        for which in range(2):
+            pltpu.make_async_copy(
+                res_ref.at[unit, :, pl.ds(0, span)], og_out.at[:, pl.ds(0, span)],
+                out_sem.at[unit, which],
+            ).wait()
+        return carry
+
+    lax.fori_loop(0, 12, saved, 0)
+
+
+def side_by_side(pick, first):
+    return jnp.concatenate([pick(first + inner) for inner in range(4)], axis=1)
+
+
+def seen(shape):
+    keys = lax.broadcasted_iota(jnp.int32, shape, 0) // BLOCK
+    return keys <= lax.broadcasted_iota(jnp.int32, shape, 1) // BLOCK
 
 
 FORWARD_EVENTS = (
-    (1, (0, 2)),
-    (4, (1, 2)),
-    (8, (0, 3)),
-    (11, (1, 3)),
-    (13, (0, 4)),
+    (0, (0, 4)),
+    (1, (1, 3)),
+    (2, (1, 4)),
+    (3, (0, 5)),
 )
-AFTER_EVENTS = ((1, 4),)
-FIRST_TICK = 1
+TICKS = ((1, 1), (1, 1), (1, 0), (1, 0), (1,))
+SPLITS = (0, 1, 4)
 
 
 def rope_constants(blocks):
@@ -1258,42 +1385,38 @@
         pltpu.VMEM((units, deep // 2, span), low),
         pltpu.VMEM((units, steps, deep // 2 // planes, span), low),
         pltpu.VMEM((units, deep, width), low),
-        pltpu.VMEM((2, deep, span), high),
+        pltpu.VMEM((2 * blocks, 8, width), high),
     ]
     sems = [
-        (5,), (2,), (2,), (5, 4), (5, 4),
+        (5,), (2,), (2,), (6, 4), (6, 4),
         (heads,), (blocks,), (blocks,), (heads,),
-        (heads,), (blocks,), (blocks,), (heads,),
+        (heads,), (blocks,), (blocks, 2), (heads, 2),
         (units, 2), (units, 2), (units,), (units,), (units,), (units,),
         (units, steps), (units, steps), (units, steps), (units, steps),
-        (units,), (units,), (units,), (units,), (planes + 2,), (planes + 2,), (2,),
+        (units,), (units,), (units,), (units,), (planes + 2,), (planes + 2,), (units, 2),
     ]
     scratch += [dma(shape) for shape in sems] + [pltpu.SemaphoreType.REGULAR]
-    result, input_grad, table, g_qkv, g_out, g_up, g_down = pl.pallas_call(
+    result, input_grad, eds, sds, *sums = pl.pallas_call(
         functools.partial(layer_kernel, blocks, heads),
         out_shape=[
             jax.ShapeDtypeStruct((rows, width), high),
             jax.ShapeDtypeStruct((rows, width), high),
-            jax.ShapeDtypeStruct((2 * blocks, 8, width), high),
+            jax.ShapeDtypeStruct((6 * blocks, deep), low),
+            jax.ShapeDtypeStruct((6 * blocks, 4 * width), low),
         ]
-        + [jax.ShapeDtypeStruct(w.shape, high) for w in (w_qkv, w_out, w_up, w_down)],
+        + [jax.ShapeDtypeStruct(w.shape, low) for w in (w_qkv, w_out, w_up, w_down)],
         in_specs=[vmem] * 4 + [hbm] * 5,
-        out_specs=[vmem] * 3 + [hbm] * 4,
+        out_specs=[vmem] * 4 + [hbm] * 4,
         scratch_shapes=scratch,
         compiler_params=pltpu.CompilerParams(
             collective_id=1, has_side_effects=True, vmem_limit_bytes=VMEM_LIMIT
         ),
     )(tokens[0], cotangent[0], emb_rows, jnp.asarray(rope_constants(blocks)),
       w_ada, w_qkv, w_out, w_up, w_down)
-    shard_width = width // 2
-    embedded_part = lax.dynamic_slice_in_dim(
-        table[:, 4], lax.axis_index("fsdp") * shard_width, shard_width, 1
-    )
     ada_total = lax.dot_general(
-        embedded_part, table[:, :4].reshape(2 * blocks, 4 * width), (((0,), (0,)), ((), ())),
-        precision=lax.Precision.HIGHEST,
-    )
-    return (result[None], input_grad[None], g_qkv, g_out, g_up, g_down, ada_total)
+        eds, sds, (((0,), (0,)), ((), ())), preferred_element_type=jnp.float32
+    )
+    return (result[None], input_grad[None], *[total.astype(high) for total in sums], ada_total)
 
 
 def solution(mesh):

time: 343 us -> 277 us (0.81)
  Pallas kernels: 318 us -> 258 us
  local copies, waits for them, and re-layouts: 15 us -> 3.19 us
  other arithmetic: 0.76 us -> 10.4 us
    pallas_call x1, Pallas kernels: 318 us -> 258 us  [fast_device(): pl.pallas_call(functools.partial(layer_kernel, blocks, heads), out_shape=...]
    convert_element_type x0 -> x4, other arithmetic: none -> 9.61 us  [fast_device(): total.astype(high)]
    unnamed x23 -> x16, local copies, waits for them, and re-layouts: 11.8 us -> 2.58 us
where the time goes in v3:
time: 277 us; the launch traced here: 276 us
  Pallas kernels  258 us (93%)
  other arithmetic  10.4 us (4%)
  local copies, waits for them, and re-layouts  3.19 us (1%)
  matrix products  2.98 us (1%)
    pallas_call x1, Pallas kernels, fast_device(): pl.pallas_call(functools.partial(layer_kernel, blocks, heads), out_shape=...  258 us
    convert_element_type x4, other arithmetic, fast_device(): total.astype(high)  9.61 us

profile of v3, /device:TPU:1, one launch (start us, length us, event | category | flops | bytes accessed | tf_op | source)
XLA Modules:
  0.0 276.3 jit_solution(9527075010297129485)
XLA Ops:
  1.3 0.8 convert_reduce_fusion
  2.0 0.6 broadcast_in_dim.18.emb_ref
  2.7 258.4 %shard_map.153 = (f32[256,768]{1,0:T(8,128)}, f32[256,768]{1,0:T(8,128)}, bf16[96,384]{1,0:T(8,128)(2,1)}, bf16[96,3072]{1,0:T(8,128)(2,1)}, bf16[384,2304]{1,0:...) custom-call(bf16[256,768]{1,0:T(8,128)(2,1)} %bitcast.12, ...), custom_call_target="tpu_custom_call" | custom-call | tf_op jit(solution)/shard_map/pallas_call | solution.py:1399
  261.1 0.0 copy-start.2
  261.1 2.3 convert_element_type.18
  263.4 0.0 copy-done.2
  263.4 0.0 copy-start.1
  263.4 2.0 convert_element_type.17
  265.4 0.8 copy-done.1
  266.2 0.0 copy-start
  266.2 2.8 convert_element_type.19
  269.0 0.0 copy-done
  269.0 0.0 copy-start.5
  269.0 0.0 copy-start.6
  269.0 2.5 convert_element_type.20
  271.5 0.0 copy-done.5
  271.5 0.0 copy-done.6
  271.5 0.0 copy-start.4
  271.5 0.0 copy-start.3
  271.5 3.0 %fusion = f32[384,3072]{1,0:T(8,128)} fusion(bf16[96,384]{1,0:T(8,128)(2,1)S(1)} %copy-done.6, bf16[96,3072]{1,0:T(8,128)(2,1)S(1)} %copy-done.5), kind=kOutput, calls=%fused_computation.1 | convolution fusion | flops 226492416 | bytes 5382144 | tf_op jit(solution)/shard_map/dot_general | solution.py:1416
  274.5 0.0 copy-done.4
  274.5 0.9 copy.20
  275.4 0.0 copy-done.3
  275.4 0.9 copy.21
Async XLA Ops:
  261.1 2.3 copy-start.2
  263.4 2.8 %copy-start.1 = (bf16[384,3072]{1,0:T(8,128)(2,1)S(1)}, bf16[384,3072]{1,0:T(8,128)(2,1)}, u32[]{:S(2)}) copy-start(bf16[384,3072]{1,0:T(8,128)(2,1)} %get-tuple-element.19) | copy-start | bytes 7077892
  266.2 2.8 %copy-start = (bf16[1536,768]{1,0:T(8,128)(2,1)S(1)}, bf16[1536,768]{1,0:T(8,128)(2,1)}, u32[]{:S(2)}) copy-start(bf16[1536,768]{1,0:T(8,128)(2,1)} %get-tuple-element.20) | copy-start | bytes 7077892
  269.0 2.6 copy-start.5
  269.0 2.6 copy-start.6
  271.5 3.0 %copy-start.4 = (f32[256,768]{1,0:T(8,128)S(1)}, f32[256,768]{1,0:T(8,128)}, u32[]{:S(2)}) copy-start(f32[256,768]{1,0:T(8,128)} %get-tuple-element.15) | copy-start | bytes 2359300
  271.5 3.9 %copy-start.3 = (f32[256,768]{1,0:T(8,128)S(1)}, f32[256,768]{1,0:T(8,128)}, u32[]{:S(2)}) copy-start(f32[256,768]{1,0:T(8,128)} %get-tuple-element.16) | copy-start | bytes 2359300

commit v4 on v3

--- a/solution.py
+++ b/solution.py
@@ -11,7 +11,7 @@
 
 HD = 64
 BLOCK = 256
-VMEM_LIMIT = 62 * 1024 * 1024
+VMEM_LIMIT = 63 * 1024 * 1024
 MESH = pl.DeviceIdType.MESH
 
 
@@ -464,7 +464,7 @@
     wq, wo, wu, wd, mod_ref, emb_other, part_other, part_send,
     hid1_t, mid_ref, ap_ref, sums_ref, cos_ref, sin_ref,
     qs_ref, buf_ref, mix_ref, lse_ref, att_ref, douts_ref, got_ref,
-    parts, sib_ref, row_ref, x_ref, z_ref, res_ref, table_ref,
+    parts, sib_ref, row_ref, x_ref, z_ref, line_ref, res_ref, table_ref,
     own_sem, small_send, small_recv, w_send, w_recv,
     fs, fr, fbs, fbr, bs, br, bbs, bbr,
     s_sib, r_sib, s_row, r_row, s_x, r_x, s_z, r_z, s_az, r_az, s_ax, r_ax, s_as, r_as,
@@ -505,14 +505,14 @@
         (0, 0, third),
         (0, third, third),
         (0, 2 * third, third),
-        (1, 0, quarter_rows[1]),
-        (2, 0, quarter_rows[2]),
+        (1, 0, 2 * quarter_rows[1]),
+        (2, 0, 2 * quarter_rows[2]),
         (3, 0, 2 * quarter_rows[3]),
     ]
 
     def chunk_start(index, half, which):
         weight, first, count = chunks[index]
-        if index == 5:
+        if index > 2:
             return pl.multiple_of(half * 2 * count + lax.rem(which, 2) * count, 16)
         return pl.multiple_of((half * 4 + which) * quarter_rows[weight] + first, 16)
 
@@ -534,7 +534,7 @@
 
     def pass_on(index):
         landed(chunk_ref(index, piece), w_recv.at[index, 0])
-        if index < 5:
+        if index < 3:
             onward(index, piece, 1, chip_next).start()
         onward(index, piece, 2, sibling).start()
 
@@ -545,13 +545,13 @@
 
     def chunk_done(index):
         landed(chunk_ref(index, jnp.bitwise_xor(piece, 1)), w_recv.at[index, 2])
-        if index < 5:
+        if index < 3:
             landed(chunk_ref(index, jnp.bitwise_xor(piece, 3)), w_recv.at[index, 3])
 
     def chunk_sent(index):
         y_copy(index).wait_send()
         onward(index, piece, 2, sibling).wait_send()
-        if index < 5:
+        if index < 3:
             onward(index, piece, 1, chip_next).wait_send()
             onward(index, jnp.bitwise_xor(piece, 2), 3, sibling).wait_send()
 
@@ -564,7 +564,7 @@
 
     emb_copy = remote(emb_ref, emb_other, small_send.at[0], small_recv.at[0], fsdp=other)
     emb_copy.start()
-    for index in range(5):
+    for index in range(3):
         y_copy(index).start()
 
     def opening(ada_ref, hid1):
@@ -584,6 +584,8 @@
         part_send[...] = partial[8:]
         part_copy = remote(part_send, part_other, small_send.at[1], small_recv.at[1], fsdp=other)
         part_copy.start()
+        for index in (3, 4, 5):
+            y_copy(index).start()
         pass_on(0)
         lanes = lax.broadcasted_iota(jnp.int32, (HD // 2, 128), 1)
         pick = lanes == me
@@ -639,8 +641,6 @@
             return carry
 
         lax.fori_loop(0, heads, send_block, 0)
-        y_copy(5).start()
-        pass_on(3)
 
     def send_head(which, source, target, send_sem, recv_sem):
         goal = head_owner(which)
@@ -719,14 +719,15 @@
             def _():
                 attend(group)
 
-            for when, event in FORWARD_EVENTS:
+            for when in range(2):
                 @pl.when(group == when)
-                def _(event=event):
-                    (pass_on, pass_last)[event[0]](event[1])
+                def _(when=when):
+                    pass_on(3 + when)
 
             return carry
 
         lax.fori_loop(0, blocks // 4, visit, 0)
+        pass_on(5)
 
         @pl.when(owner)
         def _():
@@ -784,7 +785,7 @@
                 goal = lax.rem(plane + step, planes)
                 rows = pl.ds(pl.multiple_of(goal * small, 16), small)
                 copies.append(
-                    remote(x_ref.at[unit, rows], z_ref.at[unit, step - 1],
+                    remote(x_ref.at[unit, rows], z_ref.at[unit - 9, step - 1],
                            s_z.at[unit, step - 1], r_z.at[unit, step - 1], ctx=4 * goal + piece)
                 )
             return copies
@@ -879,14 +880,17 @@
                 x_ref[unit, spot, :] = value
 
             add_into(put, lambda spot: x_ref[unit, spot, :], lambda spot: ref[spot, :], half_deep)
+
+        def stage3_direct(unit):
+            stage3(unit)
             launch(to_z(unit))
 
         def stage4(unit):
             rows = pl.ds(pl.multiple_of(plane * small, 16), small)
             total = x_ref[unit, rows, :].astype(jnp.float32)
             for step in range(1, planes):
-                landed(z_ref.at[unit, step - 1], r_z.at[unit, step - 1])
-                total += z_ref[unit, step - 1].astype(jnp.float32)
+                landed(z_ref.at[unit - 9, step - 1], r_z.at[unit, step - 1])
+                total += z_ref[unit - 9, step - 1].astype(jnp.float32)
             spots = pl.ds(pl.multiple_of(xbit * half_deep + plane * small, 16), small)
             res_ref[unit, spots, mine] = total.astype(jnp.bfloat16)
             launch(along_z(unit))
@@ -902,38 +906,127 @@
             launch(along_s(unit))
             write_out(unit, 0, mine)
 
-        def stage7(unit):
+        line_rows = half_deep // 2
+
+        def line_spots(way):
+            return pl.ds(way * line_rows, line_rows)
+
+        def line_slab(unit, way):
+            rows = pl.ds(pl.multiple_of(xbit * half_deep + way * line_rows, 16), line_rows)
+            return res_ref.at[unit, rows, mine]
+
+        def line_sum(unit, way):
+            goal = me - 4 if way == 0 else me + 4
+            return remote(x_ref.at[unit, line_spots(way)], line_ref.at[unit, way],
+                          s_z.at[unit, way], r_z.at[unit, way], ctx=goal)
+
+        def line_back(unit, way):
+            goal = me + 4 if way == 0 else me - 4
+            return remote(line_slab(unit, way), line_slab(unit, way),
+                          s_az.at[unit, way], r_az.at[unit, way], ctx=goal)
+
+        def line_place(way):
+            return planes - 1 - plane if way == 0 else plane
+
+        def line_add(unit, way):
+            landed(line_ref.at[unit, way], r_z.at[unit, way])
+            total = x_ref[unit, line_spots(way), :].astype(jnp.float32)
+            return (total + line_ref[unit, way].astype(jnp.float32)).astype(jnp.bfloat16)
+
+        def towards(hop):
+            def stage(unit):
+                if hop == 0:
+                    stage3(unit)
+                for way in range(2):
+                    @pl.when(line_place(way) == hop)
+                    def _(way=way):
+                        if hop == planes - 1:
+                            line_slab(unit, way)[...] = line_add(unit, way)
+                            line_back(unit, way).start()
+                            return
+                        if hop:
+                            x_ref[unit, line_spots(way), :] = line_add(unit, way)
+                        line_sum(unit, way).start()
+
+            return stage
+
+        def homewards(hop):
+            def stage(unit):
+                for way in range(2):
+                    @pl.when(line_place(way) == planes - 1 - hop)
+                    def _(way=way):
+                        landed(line_slab(unit, way), r_az.at[unit, way])
+                        if hop < planes - 1:
+                            line_back(unit, way).start()
+
+                if hop == planes - 1:
+                    launch(along_x(unit))
+
+            return stage
+
+        def close(unit):
             landed(res_ref.at[unit, :, theirs], r_as.at[unit])
             write_out(unit, 1, theirs)
-            for make in (to_x, to_z, along_z, along_x, along_s):
+            for make in (to_x, along_x, along_s):
                 for copy in make(unit):
                     copy.wait_send()
 
-        return stage0, stage1, stage2, stage3, stage4, stage5, stage6, stage7
+        def line_close(unit):
+            close(unit)
+            for way in range(2):
+                @pl.when(line_place(way) < planes - 1)
+                def _(way=way):
+                    line_sum(unit, way).wait_send()
+
+                @pl.when(line_place(way) > 0)
+                def _(way=way):
+                    line_back(unit, way).wait_send()
+
+        def stage7(unit):
+            close(unit)
+            for make in (to_z, along_z):
+                for copy in make(unit):
+                    copy.wait_send()
+
+        line = [towards(hop) for hop in range(planes)]
+        line += [homewards(hop) for hop in range(1, planes)]
+        direct = [stage3_direct, stage4, stage5, stage6, stage7]
+        return stage0, stage1, stage2, line + [stage6, line_close], direct
 
     early = pipeline(part_of, sib_of)
     late = pipeline(qkv_part, qkv_sib)
 
     def tick(time, carry):
-        for stage, lag in ((1, 0), (2, 2)):
-            unit = time - lag
+        @pl.when((time >= 0) & (time < 9))
+        def _():
+            early[2](time)
+
+        @pl.when((time >= 9) & (time < 12))
+        def _():
+            late[2](time)
+
+        for lag, stage in enumerate(early[3]):
+            unit = time - lag - 1
 
             @pl.when((unit >= 0) & (unit < 9))
             def _(stage=stage, unit=unit):
-                early[stage](unit)
+                stage(unit)
+
+        for lag, stage in enumerate(late[4]):
+            unit = time - lag - 1
 
             @pl.when((unit >= 9) & (unit < 12))
             def _(stage=stage, unit=unit):
-                late[stage](unit)
-
-        for stage in range(3, 8):
-            unit = time - stage
-
-            @pl.when((unit >= 0) & (unit < 12))
-            def _(stage=stage, unit=unit):
-                early[stage](unit)
+                stage(unit)
 
         return carry
+
+    def begin(stages, first, last):
+        def one(unit, carry):
+            stages[1](unit)
+            return carry
+
+        lax.fori_loop(first, last, one, 0)
 
     def ticks(first, last):
         lax.fori_loop(first, last, tick, 0)
@@ -999,6 +1092,7 @@
                 acc_ref[...] += product_back(grad_pre, wu[:, cols])
             for pick in range(4):
                 early[0](4 * index + pick)
+            begin(early, 0, 4 * index)
             return carry
 
         lax.fori_loop(0, 2, down, 0)
@@ -1023,13 +1117,14 @@
             send_head(lax.rem(step + 3 * (plane + 2), heads), douts_ref, got_ref, bs, br)
             return carry
 
-        early[1](0)
         lax.fori_loop(0, heads, send_dout, 0)
-        early[1](1)
+        begin(early, 4, 8)
         grad_out = product(att_ref[...].reshape(width, BLOCK), low_ref[...]).astype(jnp.bfloat16)
         parts[8, 0] = grad_out[:deep]
         parts[8, 1] = grad_out[deep:]
         early[0](8)
+        begin(early, 8, 9)
+        ticks(0, FIRST_TICKS)
 
     pl.run_scoped(
         middle_part,
@@ -1111,23 +1206,28 @@
                     bbr.at[head, slot],
                 ).start()
 
-        begun = 2
-        for inner in range(4):
-            def visit(group, carry, inner=inner):
-                @pl.when(owner)
-                def _():
-                    key_back(group, inner)
-
-                return carry
-
-            for edge in range(len(TICKS[inner])):
-                low, high = SPLITS[edge], SPLITS[edge + 1]
-                lax.fori_loop(low, high, visit, 0)
-                ticks(begun, begun + TICKS[inner][edge])
-                begun += TICKS[inner][edge]
-
-        @pl.when(owner)
-        def _():
+        def visit(step, carry):
+            for inner in range(4):
+                for edge in range(len(SPLITS) - 1):
+                    @pl.when(owner & (step == (len(SPLITS) - 1) * inner + edge))
+                    def _(inner=inner, edge=edge):
+                        def one(group, carry):
+                            key_back(group, inner)
+                            return carry
+
+                        lax.fori_loop(SPLITS[edge], SPLITS[edge + 1], one, 0)
+
+            low = sum(jnp.where(step > index, count, 0) for index, count in enumerate(TICKS))
+            high = sum(jnp.where(step >= index, count, 0) for index, count in enumerate(TICKS))
+            ticks(low + FIRST_TICKS, high + FIRST_TICKS)
+
+            @pl.when(owner & (step == len(TICKS) - 2))
+            def _():
+                finish_queries()
+
+            return carry
+
+        def finish_queries():
             def finish_query(group, carry):
                 grad_query = (grad_ref[group] * score_scale).astype(jnp.bfloat16)
                 for inner in range(4):
@@ -1138,7 +1238,7 @@
 
             lax.fori_loop(0, blocks // 4, finish_query, 0)
 
-        ticks(begun, begun + TICKS[4][0])
+        lax.fori_loop(0, len(TICKS), visit, 0)
 
         @pl.when(owner)
         def _():
@@ -1209,6 +1309,7 @@
             acc_ref[...] += product_back(gproj[:, cols], wq[:, cols])
             return carry
 
+        begin(late, 9, 12)
         lax.fori_loop(0, 3, back, 0)
         normed, inverse = layer_norm(tok_ref[...].astype(jnp.float32))
         grad_hidden = acc_ref[...]
@@ -1255,7 +1356,7 @@
     for copy in table_row():
         copy.start()
 
-    begun = 2 + sum(sum(counts) for counts in TICKS)
+    begun = FIRST_TICKS + sum(TICKS)
 
     def finish(time, carry):
         tick(time, carry)
@@ -1282,7 +1383,7 @@
 
         return carry
 
-    lax.fori_loop(begun, 19, finish, 0)
+    lax.fori_loop(begun, 9 + len(early[3]), finish, 0)
     landed(slots((1 - core) * 4 * planes, 4 * planes), r_t.at[2])
     count = 2 * blocks
     emb_cols = pl.ds(pl.multiple_of(row * (width // 2), 128), width // 2)
@@ -1321,13 +1422,8 @@
     return keys <= lax.broadcasted_iota(jnp.int32, shape, 1) // BLOCK
 
 
-FORWARD_EVENTS = (
-    (0, (0, 4)),
-    (1, (1, 3)),
-    (2, (1, 4)),
-    (3, (0, 5)),
-)
-TICKS = ((1, 1), (1, 1), (1, 0), (1, 0), (1,))
+FIRST_TICKS = 1
+TICKS = (1, 1, 1, 1, 1, 0, 1, 0, 2)
 SPLITS = (0, 1, 4)
 
 
@@ -1383,7 +1479,8 @@
         pltpu.VMEM((9, 2, deep, span), low),
         pltpu.VMEM((units, deep, span), low),
         pltpu.VMEM((units, deep // 2, span), low),
-        pltpu.VMEM((units, steps, deep // 2 // planes, span), low),
+        pltpu.VMEM((3, steps, deep // 2 // planes, span), low),
+        pltpu.VMEM((9, 2, deep // 4, span), low),
         pltpu.VMEM((units, deep, width), low),
         pltpu.VMEM((2 * blocks, 8, width), high),
     ]

time: 277 us -> 256 us (0.924)
  Pallas kernels: 258 us -> 237 us
    pallas_call x1, Pallas kernels: 258 us -> 237 us  [fast_device(): pl.pallas_call(functools.partial(layer_kernel, blocks, heads), out_shape=...]
where the time goes in v4:
time: 256 us; the launch traced here: 255 us
  Pallas kernels  237 us (93%)
  other arithmetic  10.4 us (4%)
  local copies, waits for them, and re-layouts  3.19 us (1%)
  matrix products  2.98 us (1%)
    pallas_call x1, Pallas kernels, fast_device(): pl.pallas_call(functools.partial(layer_kernel, blocks, heads), out_shape=...  237 us
    convert_element_type x4, other arithmetic, fast_device(): total.astype(high)  9.61 us

profile of v4, /device:TPU:1, one launch (start us, length us, event | category | flops | bytes accessed | tf_op | source)
XLA Modules:
  0.0 254.7 jit_solution(7230646089892086013)
XLA Ops:
  1.3 0.8 convert_reduce_fusion
  2.0 0.6 broadcast_in_dim.18.emb_ref
  2.7 236.8 %shard_map.153 = (f32[256,768]{1,0:T(8,128)}, f32[256,768]{1,0:T(8,128)}, bf16[96,384]{1,0:T(8,128)(2,1)}, bf16[96,3072]{1,0:T(8,128)(2,1)}, bf16[384,2304]{1,0:...) custom-call(bf16[256,768]{1,0:T(8,128)(2,1)} %bitcast.12, ...), custom_call_target="tpu_custom_call" | custom-call | tf_op jit(solution)/shard_map/pallas_call | solution.py:1496
  239.5 0.0 copy-start.2
  239.5 2.3 convert_element_type.18
  241.8 0.0 copy-done.2
  241.8 0.0 copy-start.1
  241.8 2.0 convert_element_type.17
  243.8 0.8 copy-done.1
  244.6 0.0 copy-start
  244.6 2.8 %convert_element_type.19 = f32[384,3072]{1,0:T(8,128)} convert(bf16[384,3072]{1,0:T(8,128)(2,1)S(1)} %copy-done.1) | non-fusion elementwise | flops 1179648 | bytes 7077888 | tf_op jit(solution)/shard_map/convert_element_type | solution.py:1516
  247.4 0.0 copy-done
  247.4 0.0 copy-start.5
  247.4 0.0 copy-start.6
  247.4 2.5 convert_element_type.20
  249.9 0.0 copy-done.5
  249.9 0.0 copy-done.6
  249.9 0.0 copy-start.4
  249.9 0.0 copy-start.3
  249.9 3.0 %fusion = f32[384,3072]{1,0:T(8,128)} fusion(bf16[96,384]{1,0:T(8,128)(2,1)S(1)} %copy-done.6, bf16[96,3072]{1,0:T(8,128)(2,1)S(1)} %copy-done.5), kind=kOutput, calls=%fused_computation.1 | convolution fusion | flops 226492416 | bytes 5382144 | tf_op jit(solution)/shard_map/dot_general | solution.py:1513
  252.9 0.0 copy-done.4
  252.9 0.9 copy.20
  253.8 0.0 copy-done.3
  253.8 0.9 copy.21
Async XLA Ops:
  239.5 2.3 copy-start.2
  241.8 2.8 %copy-start.1 = (bf16[384,3072]{1,0:T(8,128)(2,1)S(1)}, bf16[384,3072]{1,0:T(8,128)(2,1)}, u32[]{:S(2)}) copy-start(bf16[384,3072]{1,0:T(8,128)(2,1)} %get-tuple-element.19) | copy-start | bytes 7077892
  244.6 2.8 %copy-start = (bf16[1536,768]{1,0:T(8,128)(2,1)S(1)}, bf16[1536,768]{1,0:T(8,128)(2,1)}, u32[]{:S(2)}) copy-start(bf16[1536,768]{1,0:T(8,128)(2,1)} %get-tuple-element.20) | copy-start | bytes 7077892
  247.4 2.6 %copy-start.5 = (bf16[96,3072]{1,0:T(8,128)(2,1)S(1)}, bf16[96,3072]{1,0:T(8,128)(2,1)}, u32[]{:S(2)}) copy-start(bf16[96,3072]{1,0:T(8,128)(2,1)} %get-tuple-element.22) | copy-start | bytes 1769476
  247.4 2.6 %copy-start.6 = (bf16[96,384]{1,0:T(8,128)(2,1)S(1)}, bf16[96,384]{1,0:T(8,128)(2,1)}, u32[]{:S(2)}) copy-start(bf16[96,384]{1,0:T(8,128)(2,1)} %get-tuple-element.21) | copy-start | bytes 221188
  249.9 3.0 %copy-start.4 = (f32[256,768]{1,0:T(8,128)S(1)}, f32[256,768]{1,0:T(8,128)}, u32[]{:S(2)}) copy-start(f32[256,768]{1,0:T(8,128)} %get-tuple-element.15) | copy-start | bytes 2359300
  249.9 3.9 %copy-start.3 = (f32[256,768]{1,0:T(8,128)S(1)}, f32[256,768]{1,0:T(8,128)}, u32[]{:S(2)}) copy-start(f32[256,768]{1,0:T(8,128)} %get-tuple-element.16) | copy-start | bytes 2359300

commit v5 on v4

--- a/solution.py
+++ b/solution.py
@@ -11,7 +11,7 @@
 
 HD = 64
 BLOCK = 256
-VMEM_LIMIT = 63 * 1024 * 1024
+VMEM_LIMIT = 65152 * 1024
 MESH = pl.DeviceIdType.MESH
 
 
@@ -1388,8 +1388,7 @@
     count = 2 * blocks
     emb_cols = pl.ds(pl.multiple_of(row * (width // 2), 128), width // 2)
     eds = table_ref[:, 4, emb_cols].astype(jnp.bfloat16)
-    for third_part in range(3):
-        eds_ref[third_part * count : (third_part + 1) * count, :] = eds
+    eds_ref[...] = transposed(jnp.concatenate([eds] * 3, axis=0))
     for index in range(4):
         left = table_ref[:, index, :]
         for third_part in range(3):
@@ -1425,6 +1424,40 @@
 FIRST_TICKS = 1
 TICKS = (1, 1, 1, 1, 1, 0, 1, 0, 2)
 SPLITS = (0, 1, 4)
+
+
+def widen_kernel(*refs):
+    lows, eds_ref, sds_ref = refs[2:6], refs[6], refs[7]
+    outs = refs[8:]
+    for source, target in zip(refs[:2], outs[:2]):
+        target[...] = source[...]
+    for source, target in zip(lows, outs[2:6]):
+        target[...] = source[...].astype(jnp.float32)
+    outs[6][...] = product(eds_ref[...], sds_ref[...])
+
+
+def widen(result, input_grad, sums, eds, sds):
+    steps = WIDEN_STEPS
+
+    def rows_of(array):
+        return pl.BlockSpec((array.shape[0] // steps, array.shape[1]), lambda index: (index, 0))
+
+    ada = jax.ShapeDtypeStruct((eds.shape[0], sds.shape[1]), jnp.float32)
+    arrays = [result, input_grad, *sums]
+    outs = [jax.ShapeDtypeStruct(array.shape, jnp.float32) for array in arrays] + [ada]
+    got = pl.pallas_call(
+        widen_kernel,
+        grid=(steps,),
+        out_shape=outs,
+        in_specs=[rows_of(array) for array in arrays]
+        + [rows_of(eds), pl.BlockSpec(sds.shape, lambda index: (0, 0))],
+        out_specs=[rows_of(array) for array in outs],
+        compiler_params=pltpu.CompilerParams(vmem_limit_bytes=VMEM_LIMIT),
+    )(*arrays, eds, sds)
+    return got[0], got[1], got[2:6], got[6]
+
+
+WIDEN_STEPS = 4
 
 
 def rope_constants(blocks):
@@ -1498,7 +1531,7 @@
         out_shape=[
             jax.ShapeDtypeStruct((rows, width), high),
             jax.ShapeDtypeStruct((rows, width), high),
-            jax.ShapeDtypeStruct((6 * blocks, deep), low),
+            jax.ShapeDtypeStruct((deep, 6 * blocks), low),
             jax.ShapeDtypeStruct((6 * blocks, 4 * width), low),
         ]
         + [jax.ShapeDtypeStruct(w.shape, low) for w in (w_qkv, w_out, w_up, w_down)],
@@ -1510,10 +1543,8 @@
         ),
     )(tokens[0], cotangent[0], emb_rows, jnp.asarray(rope_constants(blocks)),
       w_ada, w_qkv, w_out, w_up, w_down)
-    ada_total = lax.dot_general(
-        eds, sds, (((0,), (0,)), ((), ())), preferred_element_type=jnp.float32
-    )
-    return (result[None], input_grad[None], *[total.astype(high) for total in sums], ada_total)
+    result, input_grad, totals, ada_total = widen(result, input_grad, sums, eds, sds)
+    return (result[None], input_grad[None], *totals, ada_total)
 
 
 def solution(mesh):

time: 256 us -> 252 us (0.984)
  Pallas kernels: 237 us -> 248 us
  other arithmetic: 10.4 us -> 0.76 us
  matrix products: 2.98 us -> 0 us
  local copies, waits for them, and re-layouts: 3.19 us -> 0.61 us
    pallas_call x0 -> x1, Pallas kernels: none -> 10.8 us  [widen(): pl.pallas_call(widen_kernel, grid=(steps,), out_shape=outs, in_specs=[row...]
    convert_element_type x4 -> x0, other arithmetic: 9.61 us -> none  [fast_device(): total.astype(high)]
    dot_general x1 -> x0, matrix products: 2.98 us -> none  [fast_device(): lax.dot_general(eds, sds, (((0,), (0,)), ((), ())), preferred_element_typ...]
    unnamed x16 -> x0, local copies, waits for them, and re-layouts: 2.58 us -> none
where the time goes in v5:
time: 252 us; the launch traced here: 251 us
  Pallas kernels  248 us (98%)
    pallas_call x1, Pallas kernels, fast_device(): pl.pallas_call(functools.partial(layer_kernel, blocks, heads), out_shape=...  237 us
    pallas_call x1, Pallas kernels, widen(): pl.pallas_call(widen_kernel, grid=(steps,), out_shape=outs, in_specs=[row...  10.8 us

profile of v5, /device:TPU:1, one launch (start us, length us, event | category | flops | bytes accessed | tf_op | source)
XLA Modules:
  0.0 250.9 jit_solution(5550079530073863255)
XLA Ops:
  1.3 0.8 convert_reduce_fusion
  2.0 0.6 broadcast_in_dim.18.emb_ref
  2.7 237.3 %shard_map.153 = (f32[256,768]{1,0:T(8,128)}, f32[256,768]{1,0:T(8,128)}, bf16[384,96]{1,0:T(8,128)(2,1)}, bf16[96,3072]{1,0:T(8,128)(2,1)}, bf16[384,2304]{1,0:...) custom-call(bf16[256,768]{1,0:T(8,128)(2,1)} %bitcast.8, ...), custom_call_target="tpu_custom_call" | custom-call | tf_op jit(solution)/shard_map/pallas_call | solution.py:1529
  239.9 10.8 %shard_map.154 = (f32[256,768]{1,0:T(8,128)}, f32[256,768]{1,0:T(8,128)}, f32[384,2304]{1,0:T(8,128)}, f32[384,768]{1,0:T(8,128)}, f32[384,3072]{1,0:T(8,128)}, ...) custom-call(f32[256,768]{1,0:T(8,128)} %get-tuple-element.22.refs_0_, f32[256,768]{1,0:T(8,128)} %get-tuple-element.23.refs_1_, ...), custom_call_target="tpu_custom_call" | custom-call | tf_op jit(solution)/shard_map/pallas_call | solution.py:1448

commit v6 on v5

--- a/solution.py
+++ b/solution.py
@@ -997,6 +997,20 @@
     late = pipeline(qkv_part, qkv_sib)
 
     def tick(time, carry):
+        for lag, stage in enumerate(early[3]):
+            unit = time - lag - 1
+
+            @pl.when((unit >= 0) & (unit < 9))
+            def _(stage=stage, unit=unit):
+                stage(unit)
+
+        for lag, stage in enumerate(late[4]):
+            unit = time - lag - 1
+
+            @pl.when((unit >= 9) & (unit < 12))
+            def _(stage=stage, unit=unit):
+                stage(unit)
+
         @pl.when((time >= 0) & (time < 9))
         def _():
             early[2](time)
@@ -1004,20 +1018,6 @@
         @pl.when((time >= 9) & (time < 12))
         def _():
             late[2](time)
-
-        for lag, stage in enumerate(early[3]):
-            unit = time - lag - 1
-
-            @pl.when((unit >= 0) & (unit < 9))
-            def _(stage=stage, unit=unit):
-                stage(unit)
-
-        for lag, stage in enumerate(late[4]):
-            unit = time - lag - 1
-
-            @pl.when((unit >= 9) & (unit < 12))
-            def _(stage=stage, unit=unit):
-                stage(unit)
 
         return carry
 
@@ -1300,6 +1300,7 @@
             low = product(hid1_t[...], gproj[:, cols]).astype(jnp.bfloat16)
             wd[pl.ds(pl.multiple_of(index * width, width), width), :] = low
             late[0](9 + index)
+            begin(late, 8 + jnp.maximum(index, 1), 9 + index)
             return carry
 
         lax.fori_loop(0, 3, gradient, 0)
@@ -1309,7 +1310,7 @@
             acc_ref[...] += product_back(gproj[:, cols], wq[:, cols])
             return carry
 
-        begin(late, 9, 12)
+        begin(late, 11, 12)
         lax.fori_loop(0, 3, back, 0)
         normed, inverse = layer_norm(tok_ref[...].astype(jnp.float32))
         grad_hidden = acc_ref[...]

time: 252 us -> 252 us (level)
  no operation moved by 1% of the time
where the time goes in v6:
time: 252 us; the launch traced here: 251 us
  Pallas kernels  248 us (98%)
    pallas_call x1, Pallas kernels, fast_device(): pl.pallas_call(functools.partial(layer_kernel, blocks, heads), out_shape=...  237 us
    pallas_call x1, Pallas kernels, widen(): pl.pallas_call(widen_kernel, grid=(steps,), out_shape=outs, in_specs=[row...  10.8 us

profile of v6, /device:TPU:1, one launch (start us, length us, event | category | flops | bytes accessed | tf_op | source)
XLA Modules:
  0.0 250.8 jit_solution(13411791605395042892)
XLA Ops:
  1.3 0.8 convert_reduce_fusion
  2.0 0.6 broadcast_in_dim.18.emb_ref
  2.7 237.1 %shard_map.153 = (f32[256,768]{1,0:T(8,128)}, f32[256,768]{1,0:T(8,128)}, bf16[384,96]{1,0:T(8,128)(2,1)}, bf16[96,3072]{1,0:T(8,128)(2,1)}, bf16[384,2304]{1,0:...) custom-call(bf16[256,768]{1,0:T(8,128)(2,1)} %bitcast.8, ...), custom_call_target="tpu_custom_call" | custom-call | tf_op jit(solution)/shard_map/pallas_call | solution.py:1530
  239.8 10.8 %shard_map.154 = (f32[256,768]{1,0:T(8,128)}, f32[256,768]{1,0:T(8,128)}, f32[384,2304]{1,0:T(8,128)}, f32[384,768]{1,0:T(8,128)}, f32[384,3072]{1,0:T(8,128)}, ...) custom-call(f32[256,768]{1,0:T(8,128)} %get-tuple-element.22.refs_0_, f32[256,768]{1,0:T(8,128)} %get-tuple-element.23.refs_1_, ...), custom_call_target="tpu_custom_call" | custom-call | tf_op jit(solution)/shard_map/pallas_call | solution.py:1449
